TPU v7x, 256 devices: a whole 4x4x8 slice. The times are simulated.
256 devices in a mesh: ev: 4 (over y), slab: 64 (over x, z, core).
Axes of the slice: x: 4, y: 4, z: 8, core: 2. Of those that a mesh axis runs over, the one named last changes fastest.
Arguments:
- kernels: float32 [8192, 32, 128], P(('ev', 'slab')), may hold values from -1 to 1
- block_ids: int32 [8192, 32], P(('ev', 'slab')), may hold values from 0 to 65535, as said below
- delays: float32 [8192], P(('ev', 'slab')), may hold values from -240 to 240
Outputs:
- solution: float32 [512, 128, 128], P('slab')
Inputs may be any that keep to these rules, and one draw needn't show every extreme that they name: `block_ids`: block b is column (b // 128, b % 128) and lies in slab b // 1024. Of the 1024 ids of one device's rays, exactly 16 lie in each slab; ids may repeat.
All inputs are finite; a program needn't handle non-finite values.
Results may differ from a plain program's by a relative error of at most 0.0001.
Values sent between devices are 32-bit elements; how exact they have to be, the bound alone decides.
No kernel may reach another device: no remote copies, remote signals or barrier semaphores. Data moves between devices by JAX's collectives and lax.ppermute only.
A program may use at most 64 MiB of HBM per device.

v0:
```python
import jax
import jax.numpy as jnp
from jax import lax
from jax.sharding import PartitionSpec as P

CX = 8
NY = 128
ITERS = 2


damping = 0.3
norm_epsilon = 1e-06


def with_halo(block, sides, width):
    for axis, dim in sides:
        count = lax.axis_size(axis)
        forward = [(i, i + 1) for i in range(count - 1)]
        forward.append((count - 1, 0))
        backward = [(target, source) for source, target in forward]
        low = lax.ppermute(
            lax.slice_in_dim(block, block.shape[dim] - width, None, axis=dim), axis, forward
        )
        high = lax.ppermute(lax.slice_in_dim(block, 0, width, axis=dim), axis, backward)
        block = jnp.concatenate([low, block, high], axis=dim)
    return block


def laplace_local(field_in):
    padded = with_halo(field_in, (("slab", 0),), 1)
    inner = padded[1:-1]
    beside_all = jnp.pad(inner, ((0, 0), (1, 1), (1, 1)))
    beside = padded[2:] + padded[:-2]
    beside = (
        beside
        + beside_all[:, 2:, 1:-1]
        + beside_all[:, :-2, 1:-1]
        + beside_all[:, 1:-1, 2:]
        + beside_all[:, 1:-1, :-2]
    )
    return 6.0 * inner - beside


def finish_transpose(partial_value, local_part):
    summed = lax.psum(partial_value, "ev")
    if local_part is not None:
        summed = summed + local_part
    alpha_now = jnp.sqrt(lax.psum(jnp.sum(summed * summed), "slab") + norm_epsilon)
    return (summed / alpha_now, alpha_now)


def on_device(kernels, block_ids, delays):
    slab_count = lax.axis_size("slab")
    cells_slab = CX * NY
    ray_count = kernels.shape[0]
    per_ray = kernels.shape[1]
    width = kernels.shape[2]
    entries = ray_count * per_ray
    per_slab = entries // slab_count
    flat_ids = block_ids.reshape(entries)
    ordering = jnp.argsort(flat_ids // cells_slab, stable=True)
    position = jnp.argsort(ordering, stable=True)
    ray_of = ordering // per_ray
    sorted_local = (flat_ids[ordering] % cells_slab).reshape(slab_count, per_slab)
    wanted = lax.all_to_all(sorted_local, "slab", split_axis=0, concat_axis=0, tiled=True).reshape(
        entries
    )
    kern_sorted = kernels.reshape(entries, width)[ordering]

    def ray_transpose(ray_weights):
        spread = ray_weights[ray_of]
        weighted = (kern_sorted * spread[:, None]).reshape(slab_count, per_slab, width)
        contrib = lax.all_to_all(weighted, "slab", split_axis=0, concat_axis=0, tiled=True).reshape(
            entries, width
        )
        summed = jnp.zeros((cells_slab, width), jnp.float32).at[wanted].add(contrib)
        return summed.reshape(CX, NY, width)

    data_square = lax.psum(jnp.sum(delays * delays), ("ev", "slab"))
    beta_now = jnp.sqrt(data_square + norm_epsilon)
    ray_part = delays / beta_now
    model_part = jnp.zeros((CX, NY, width), jnp.float32)
    direction, alpha_now = finish_transpose(ray_transpose(ray_part), None)
    search = direction
    solution = jnp.zeros((CX, NY, width), jnp.float32)
    phi_bar = beta_now
    rho_bar = alpha_now
    for iteration in range(ITERS):
        table = direction.reshape(cells_slab, width)
        picked = table[wanted].reshape(slab_count, per_slab, width)
        returned = lax.all_to_all(picked, "slab", split_axis=0, concat_axis=0, tiled=True).reshape(
            entries, width
        )
        entry_sums = jnp.sum(returned * kern_sorted, axis=1)
        ray_part = (
            jnp.sum(entry_sums[position].reshape(ray_count, per_ray), axis=1) - alpha_now * ray_part
        )
        model_part = damping * laplace_local(direction) - alpha_now * model_part
        ray_square = jnp.sum(ray_part * ray_part)
        model_square = jnp.sum(model_part * model_part)
        both_squares = lax.psum(ray_square, ("ev", "slab")) + lax.psum(model_square, "slab")
        beta_now = jnp.sqrt(both_squares + norm_epsilon)
        ray_part = ray_part / beta_now
        model_part = model_part / beta_now
        rho_now = jnp.sqrt(rho_bar * rho_bar + beta_now * beta_now)
        cosine = rho_bar / rho_now
        sine_part = beta_now / rho_now
        phi_now = cosine * phi_bar
        phi_bar = sine_part * phi_bar
        solution = solution + phi_now / rho_now * search
        if iteration + 1 < ITERS:
            local_part = damping * laplace_local(model_part) - beta_now * direction
            direction, alpha_now = finish_transpose(ray_transpose(ray_part), local_part)
            theta_now = sine_part * alpha_now
            rho_bar = -cosine * alpha_now
            search = direction - theta_now / rho_now * search
    return solution


def solution(mesh):
    in_specs = (P(("ev", "slab"), None, None), P(("ev", "slab"), None), P(("ev", "slab")))
    out_specs = P("slab", None, None)
    return jax.shard_map(
        on_device, mesh=mesh, in_specs=in_specs, out_specs=out_specs, check_vma=False
    )
```

profile of v0, /device:TPU:1, one launch (start us, length us, event | category | flops | bytes accessed | tf_op | source)
XLA Modules:
  0.0 1040.1 jit_solution(9689522965077744709)
XLA Ops:
  8.7 4.4 sort.31
  13.1 4.5 gather_fusion
  18.3 13.0 %all-to-all-start = ((s32[64,1,16]{2,1,0:T(1,128)}), s32[64,1,16]{2,1,0:T(1,128)S(1)}, u32[]{:S(2)}, u32[]{:S(2)}) async-start(s32[64,1,16]{2,1,0:T(1,128)} %bitcast), calls=%async_computation | async-start | bytes 65536 | tf_op jit(solution)/shard_map/all_to_all | solution.py:65
  31.3 77.8 %psum.63 = f32[]{:T(128)} all-reduce(f32[]{:T(128)} %multiply_reduce_fusion.7), channel_id=1, replica_groups=mesh['ev'=4,'slab'=64] {'ev','slab'}, use_global_device_ids=true, to_apply=%region_2.3 | all-reduce | flops 1 | bytes 8 | tf_op jit(solution)/shard_map/psum | solution.py:79
  111.2 20.1 %select_select_fusion.1 = (f32[1024]{0:T(1024)S(1)}, pred[1024]{0:T(1024)(128)(4,1)S(1)}, pred[1024]{0:T(1024)(128)(4,1)S(1)}, pred[1024]{0:T(1024)(128)(4,1)S(1...) fusion(f32[]{:T(128)} %bitcast.4, f32[]{:T(128)} %bitcast.5, ...), kind=kLoop, calls=%fused_computation.89 | loop fusion | flops 63488 | bytes 40064 | tf_op jit(solution)/shard_map/gather | solution.py:71
  131.5 2.8 gather_fusion.1
  135.3 7.8 all-to-all-start.1
  144.6 15.8 %all-to-all-done.1 = f32[64,16,128]{2,1,0:T(8,128)S(1)} async-done(((f32[64,16,128]{2,1,0:T(8,128)}), f32[64,16,128]{2,1,0:T(8,128)S(1)}, u32[]{:S(2)}, u32[]{:S(2)}) %all-to-all-start.1) | async-done | bytes 524320 | tf_op jit(solution)/shard_map/all_to_all | solution.py:73
  160.3 6.8 scatter_custom_fusion
  167.2 41.3 %all-reduce.6.cloned.1.call-done = f32[8,128,128]{2,1,0:T(8,128)} async-done(((f32[8,128,128]{2,1,0:T(8,128)}), f32[8,128,128]{2,1,0:T(8,128)}) %all-reduce.6.cloned.1.call-update) | async-done | bytes 524304 | tf_op jit(solution)/shard_map/psum | solution.py:45
  210.3 127.4 %psum.65 = f32[]{:T(128)} all-reduce(f32[]{:T(128)} %multiply_reduce_fusion.4), channel_id=1, replica_groups=mesh['ev'=4,'slab'=64] {'slab'}, use_global_device_ids=true, to_apply=%region_6.7 | all-reduce | flops 1 | bytes 8 | tf_op jit(solution)/shard_map/psum | solution.py:48
  338.5 4.0 gather_fusion.2
  342.5 6.9 all-to-all-start.2
  349.5 4.4 sort.32
  355.7 8.1 collective-permute-done
  364.9 2.2 all-to-all-done.2
  367.3 4.5 gather_fusion.3
  372.7 125.5 %psum.67 = f32[]{:T(128)} all-reduce(f32[]{:T(128)} %get-tuple-element.11), channel_id=1, replica_groups=mesh['ev'=4,'slab'=64] {'slab'}, use_global_device_ids=true, to_apply=%region_13.14 | all-reduce | flops 1 | bytes 8 | tf_op jit(solution)/shard_map/psum | solution.py:101
  498.1 73.8 %psum.66 = f32[]{:T(128)} all-reduce(f32[]{:T(128)} %multiply_reduce_fusion.6), channel_id=1, replica_groups=mesh['ev'=4,'slab'=64] {'ev','slab'}, use_global_device_ids=true, to_apply=%region_11.12 | all-reduce | flops 1 | bytes 8 | tf_op jit(solution)/shard_map/psum | solution.py:101
  574.6 20.1 %select_select_fusion = f32[1024]{0:T(1024)S(1)} fusion(pred[1024]{0:T(1024)(128)(4,1)S(1)} %get-tuple-element.44, pred[1024]{0:T(1024)(128)(4,1)S(1)} %get-tuple-element.43, pred[1024]{0:T(1024)(128)(4,1)S(1)} %get-tuple-element.42, pred[1024]{0:T(1024)(128)(4,1)S(1)} %get-tuple-element.41, pred[1024]{0:T(1024)(128)(4,1)S(1)} %get-tuple-element.40, ...), kind=kLoop, calls=%fused_computation.88 | loop fusion | flops 31744 | bytes 35968 | tf_op jit(solution)/shard_map/gather | solution.py:71
  595.0 22.6 %all_to_all.26 = f32[64,16,128]{2,1,0:T(8,128)S(1)} all-to-all(f32[64,16,128]{2,1,0:T(8,128)S(1)} %broadcast_multiply_fusion), channel_id=1, replica_groups=mesh['ev'=4,'slab'=64] {'slab'}, dimensions={0} | all-to-all | bytes 1048576 | tf_op jit(solution)/shard_map/all_to_all | solution.py:73
  617.6 6.8 scatter_custom_fusion.1
  628.2 37.3 %all-reduce.8.cloned.1.call-done = f32[8,128,128]{2,1,0:T(8,128)} async-done(((f32[8,128,128]{2,1,0:T(8,128)}), f32[8,128,128]{2,1,0:T(8,128)}) %all-reduce.8.cloned.1.call-update) | async-done | bytes 524304 | tf_op jit(solution)/shard_map/psum | solution.py:45
  665.6 2.1 multiply_reduce_fusion.1
  667.7 127.4 %psum.69 = f32[]{:T(128)} all-reduce(f32[]{:T(128)} %get-tuple-element.9), channel_id=1, replica_groups=mesh['ev'=4,'slab'=64] {'slab'}, use_global_device_ids=true, to_apply=%region_17.18 | all-reduce | flops 1 | bytes 8 | tf_op jit(solution)/shard_map/psum | solution.py:48
  795.8 4.0 gather_fusion.4
  799.8 7.7 all-to-all-start.4
  809.6 12.2 %collective-permute-done.4 = f32[1,128,128]{2,1,0:T(8,128)S(1)} collective-permute-done((f32[1,128,128]{2,1,0:T(8,128)S(1)}, f32[1,128,128]{2,1,0:T(8,128)S(1)}, u32[]{:S(2)}, u32[]{:S(2)}) %collective-permute-start.4) | collective-permute-done | bytes 65568 | tf_op jit(solution)/shard_map/ppermute | solution.py:24
  822.9 2.1 all-to-all-done.4
  826.4 4.5 gather_fusion.5
  831.7 125.6 %psum.71 = f32[]{:T(128)} all-reduce(f32[]{:T(128)} %fusion.26), channel_id=1, replica_groups=mesh['ev'=4,'slab'=64] {'slab'}, use_global_device_ids=true, to_apply=%region_23.24 | all-reduce | flops 1 | bytes 8 | tf_op jit(solution)/shard_map/psum | solution.py:101
  957.3 73.6 %psum.70 = f32[]{:T(128)} all-reduce(f32[]{:T(128)} %multiply_reduce_fusion.5), channel_id=1, replica_groups=mesh['ev'=4,'slab'=64] {'ev','slab'}, use_global_device_ids=true, to_apply=%region_21.22 | all-reduce | flops 1 | bytes 8 | tf_op jit(solution)/shard_map/psum | solution.py:101
  (65 shorter events, 24.5 us)
Async XLA Ops:
  6.5 124.9 %copy-start = (f32[32,32,128]{2,1,0:T(8,128)S(1)}, f32[32,32,128]{2,1,0:T(8,128)}, u32[]{:S(2)}) copy-start(f32[32,32,128]{2,1,0:T(8,128)} %param.3) | copy-start | bytes 1572868
  13.1 96.7 %copy-start.2 = (f32[32]{0:T(128)S(1)}, f32[32]{0:T(128)}, u32[]{:S(2)}) copy-start(f32[32]{0:T(128)} %param.5) | copy-start | bytes 388
  18.3 117.0 %all-to-all-start = ((s32[64,1,16]{2,1,0:T(1,128)}), s32[64,1,16]{2,1,0:T(1,128)S(1)}, u32[]{:S(2)}, u32[]{:S(2)}) async-start(s32[64,1,16]{2,1,0:T(1,128)} %bitcast), calls=%async_computation | async-start | bytes 65536 | tf_op jit(solution)/shard_map/all_to_all | solution.py:65
  135.3 25.1 %all-to-all-start.1 = ((f32[64,16,128]{2,1,0:T(8,128)}), f32[64,16,128]{2,1,0:T(8,128)S(1)}, u32[]{:S(2)}, u32[]{:S(2)}) async-start(f32[64,16,128]{2,1,0:T(8,128)} %broadcast_multiply_fusion.1), calls=%async_computation.1 | async-start | bytes 1048576 | tf_op jit(solution)/shard_map/all_to_all | solution.py:73
  143.1 65.4 %all-reduce.6.cloned.1.call-start = ((), (), s32[]{:S(2)}) async-start(), calls=%async_computation.5 | async-start | bytes 1048576 | tf_op jit(solution)/shard_map/psum | solution.py:45
  208.5 129.9 %copy-start.1 = (f32[8,128,128]{2,1,0:T(8,128)S(1)}, f32[8,128,128]{2,1,0:T(8,128)}, u32[]{:S(2)}) copy-start(f32[8,128,128]{2,1,0:T(8,128)} %all-reduce.6.cloned.1.call-done) | copy-start | bytes 1572868
  342.5 24.5 %all-to-all-start.2 = ((f32[64,16,128]{2,1,0:T(8,128)}), f32[64,16,128]{2,1,0:T(8,128)S(1)}, u32[]{:S(2)}, u32[]{:S(2)}) async-start(f32[64,16,128]{2,1,0:T(8,128)} %bitcast.39), calls=%async_computation.2 | async-start | bytes 1048576 | tf_op jit(solution)/shard_map/all_to_all | solution.py:91
  349.4 316.2 %all-reduce.8.cloned.1.call-start = ((), (), s32[]{:S(2)}) async-start(), calls=%async_computation.6 | async-start | bytes 1048576 | tf_op jit(solution)/shard_map/psum | solution.py:45
  353.8 9.9 collective-permute-start
  354.5 9.3 collective-permute-start.1
  624.5 3.8 collective-permute-start.2
  624.8 3.5 collective-permute-start.3
  799.8 25.2 %all-to-all-start.4 = ((f32[64,16,128]{2,1,0:T(8,128)}), f32[64,16,128]{2,1,0:T(8,128)}, u32[]{:S(2)}, u32[]{:S(2)}) async-start(f32[64,16,128]{2,1,0:T(8,128)} %bitcast.85), calls=%async_computation.4 | async-start | bytes 1048576 | tf_op jit(solution)/shard_map/all_to_all | solution.py:91
  807.5 14.3 %collective-permute-start.4 = (f32[1,128,128]{2,1,0:T(8,128)S(1)}, f32[1,128,128]{2,1,0:T(8,128)S(1)}, u32[]{:S(2)}, u32[]{:S(2)}) collective-permute-start(f32[1,128,128]{2,1,0:T(8,128)S(1)} %get-tuple-element.45), channel_id=1, source_target_pairs={{1,0},{2,1},{3,2},{4,3},{5,4},{6,5},{7,6},{8,7},{9,8},{10,9},{11,1... | collective-permute-start | bytes 196616 | tf_op jit(solution)/shard_map/ppermute | solution.py:24
  808.2 13.6 %collective-permute-start.5 = (f32[1,128,128]{2,1,0:T(8,128)S(1)}, f32[1,128,128]{2,1,0:T(8,128)S(1)}, u32[]{:S(2)}, u32[]{:S(2)}) collective-permute-start(f32[1,128,128]{2,1,0:T(8,128)S(1)} %get-tuple-element.46), channel_id=1, source_target_pairs={{0,1},{1,2},{2,3},{3,4},{4,5},{5,6},{6,7},{7,8},{8,9},{9,10},{10,1... | collective-permute-start | bytes 196616 | tf_op jit(solution)/shard_map/ppermute | solution.py:21
Sparse Core Ops, SparseCore 0:
  167.3 41.1 all-reduce.5
  624.5 41.0 all-reduce.7
where the time goes:
time: 1040 us
  blocking collectives  754 us (72%)
  waiting for transfers between devices  121 us (12%)
  other arithmetic  76.7 us (7%)
  starting transfers between devices  40.9 us (4%)
  local copies, waits for them, and re-layouts  29.4 us (3%)
  between operations  18.7 us (2%)
    psum x2, blocking collectives, finish_transpose(): lax.psum(jnp.sum(summed * summed), 'slab') + norm_epsilon  255 us
    psum x2, blocking collectives, on_device(): lax.psum(model_square, 'slab')  251 us
    psum x2, blocking collectives, on_device(): lax.psum(ray_square, ('ev', 'slab')) + lax.psum(model_square, 'slab')  147 us
    psum x2, waiting for transfers between devices, finish_transpose(): summed = lax.psum(partial_value, 'ev')  78.6 us
    psum x1, blocking collectives, on_device(): data_square = lax.psum(jnp.sum(delays * delays), ('ev', 'slab'))  77.8 us
    gather x2, other arithmetic, ray_transpose(): spread = ray_weights[ray_of]  40.2 us
    all_to_all x1, blocking collectives, ray_transpose(): lax.all_to_all(weighted, 'slab', split_axis=0, concat_axis=0, tiled=True)  22.6 us
    ppermute x3, waiting for transfers between devices, with_halo(): lax.ppermute(lax.slice_in_dim(block, 0, width, axis=dim), axis, backward)  22.3 us
  transfers between devices with their start and end apart: 12, of which 8 were waited for; matrix products, arithmetic and copies ran while one was open for 3% of the time, Pallas kernels for 0%

commit v1 on v0

v1 whole, which is shorter than its diff:
```python
import jax
import jax.numpy as jnp
from jax import lax
from jax.experimental import pallas as pl
from jax.experimental.pallas import tpu as pltpu
from jax.sharding import Mesh, PartitionSpec as P

CX = 8
NY = 128
damping = 0.3
norm_epsilon = 1e-06

F32 = jnp.float32
BF16 = jnp.bfloat16
I32 = jnp.int32

ALL = ("ev", "sx", "sz", "sc")
SLAB = ("sx", "sz", "sc")
D1 = ("sx", "sc")
D2 = ("ev", "sz")

VM = pl.BlockSpec(memory_space=pltpu.VMEM)


def iota(shape, dim):
    return lax.broadcasted_iota(I32, shape, dim)


def split2(x):
    hi = x.astype(BF16)
    return hi, (x - hi.astype(F32)).astype(BF16)


def call(body, out_shapes, scratch=(), flops=1000000, nbytes=1000000):
    outs = [jax.ShapeDtypeStruct(s, d) for s, d in out_shapes]
    return pl.pallas_call(
        body,
        out_shape=outs,
        in_specs=None,
        out_specs=[VM] * len(outs),
        scratch_shapes=list(scratch),
        compiler_params=pltpu.CompilerParams(vmem_limit_bytes=40 << 20),
        cost_estimate=pl.CostEstimate(flops=flops, bytes_accessed=nbytes, transcendentals=0),
    )


def run(body, args, out_shapes, scratch=(), flops=1000000, nbytes=1000000):
    outs = [jax.ShapeDtypeStruct(s, d) for s, d in out_shapes]
    return pl.pallas_call(
        body,
        out_shape=outs,
        in_specs=[VM] * len(args),
        out_specs=[VM] * len(outs),
        scratch_shapes=list(scratch),
        compiler_params=pltpu.CompilerParams(vmem_limit_bytes=40 << 20),
        cost_estimate=pl.CostEstimate(flops=flops, bytes_accessed=nbytes, transcendentals=0),
    )(*args)


def prep_kernel(ids_ref, b_ref, k_ref, send_ref, oh_ref):
    ids = ids_ref[...]
    slab = lax.shift_right_logical(ids, 10)
    loc = ids & 1023
    s_f = (iota((64, 1024), 0) == slab).astype(F32)
    s_b = s_f.astype(BF16)
    ra, ca = iota((128, 256), 0), iota((128, 256), 1)
    upper = jnp.where((ra < ca) | (ca >= 128), 1.0, 0.0).astype(BF16)
    stacked = jnp.concatenate([s_b[:, 128 * i : 128 * i + 128] for i in range(8)], axis=0)
    counts = jnp.dot(stacked, upper, preferred_element_type=F32)
    offset = jnp.zeros((64, 128), F32)
    ranks = []
    for i in range(8):
        block = counts[64 * i : 64 * i + 64]
        ranks.append(
            jnp.sum(
                s_f[:, 128 * i : 128 * i + 128] * (block[:, :128] + offset), axis=0, keepdims=True
            )
        )
        offset = offset + block[:, 128:]
    rank = jnp.concatenate(ranks, axis=1)
    for m in range(4):
        for r in range(4):
            pick = jnp.where(rank == float(4 * r + m), 1.0, 0.0).astype(BF16)
            oh_ref[64 * (4 * m + r) : 64 * (4 * m + r) + 64, :] = s_b * pick
    k_hi, k_lo = split2(k_ref[...])
    both = jnp.dot(
        oh_ref[...], jnp.concatenate([k_hi, k_lo], axis=1), preferred_element_type=F32
    )
    perm = both[:, :128] + both[:, 128:]
    lane_block = lax.shift_right_logical(iota((64, 128), 1), 5)
    for r in range(4):
        rows = [perm[64 * (4 * m + r) : 64 * (4 * m + r) + 64] for m in range(4)]
        for e in range(4):
            value = None
            for m in range(4):
                d = (m - e) % 4
                moved = rows[m] if d == 0 else pltpu.roll(rows[m], 32 * d, axis=1)
                value = moved if value is None else jnp.where(lane_block == m, moved, value)
            send_ref[pl.ds(320 * e + r, 64, stride=5), :] = value
    loc_i = lax.shift_right_logical(loc, 7)
    group = lax.shift_right_logical(loc_i, 1).astype(F32)
    column = ((loc_i & 1) * 128 + (loc & 127)).astype(F32)
    ray = lax.shift_right_logical(iota((1, 1024), 1), 5).astype(F32)
    b = b_ref[...]
    b_hi, rest = b.astype(BF16), None
    rest = b - b_hi.astype(F32)
    b_mid, b_lo = split2(rest)
    values = [group.astype(BF16), column.astype(BF16), ray.astype(BF16), b_hi, b_mid, b_lo]
    left = jnp.concatenate([s_b * v for v in values], axis=0)
    slot = (iota((128, 1024), 0) & 15).astype(F32)
    right = jnp.where(slot == rank, 1.0, 0.0).astype(BF16)
    info = lax.dot_general(left, right, (((1,), (1,)), ((), ())), preferred_element_type=F32)
    lane16 = lax.shift_right_logical(iota((64, 128), 1), 4)
    b_info = info[192:256] + info[256:320] + info[320:384]
    merged = jnp.where(
        lane16 == 0,
        info[0:64],
        jnp.where(lane16 == 1, info[64:128], jnp.where(lane16 == 2, info[128:192], b_info)),
    )
    for e in range(4):
        send_ref[pl.ds(320 * e + 4, 64, stride=5), :] = merged


def scatter_rows(kt_ref, j_ref, inf_ref, l_ref, weight_rows):
    for t in range(16):
        cols = slice(256 * t, 256 * t + 256)
        w_hi, w_lo = split2(kt_ref[:, cols] * weight_rows[t])
        group = inf_ref[t : t + 1, :]
        for i in range(4):
            mask = jnp.where(group == float(i), 1.0, 0.0).astype(BF16)
            l_ref[32 * i : 32 * i + 32, cols] = w_hi * mask
            l_ref[128 + 32 * i : 160 + 32 * i, cols] = w_lo * mask
    acc = lax.dot_general(
        l_ref[...], j_ref[...], (((1,), (1,)), ((), ())), preferred_element_type=F32
    )
    return acc[:128] + acc[128:]


def to_cube(flat):
    return [
        flat[32 * (i // 2) : 32 * (i // 2) + 32, 128 * (i % 2) : 128 * (i % 2) + 128]
        for i in range(8)
    ]


def gather_rays(flat, kt_ref, j_ref, inf_ref, g_ref):
    parts = jnp.concatenate(split2(flat), axis=0)
    ray_index = iota((32, 256), 0).astype(F32)
    total = jnp.zeros((32, 256), F32)
    for t in range(16):
        cols = slice(256 * t, 256 * t + 256)
        picked = jnp.dot(parts, j_ref[:, cols], preferred_element_type=F32)
        group = inf_ref[t : t + 1, :]
        value = jnp.zeros((32, 256), F32)
        for i in range(4):
            both = picked[32 * i : 32 * i + 32] + picked[128 + 32 * i : 160 + 32 * i]
            value = jnp.where(group == float(i), both, value)
        entry = jnp.sum(kt_ref[:, cols] * value, axis=0, keepdims=True)
        total = total + jnp.where(inf_ref[32 + t : 33 + t, :] == ray_index, entry, 0.0)
    for a in range(4):
        for h in range(2):
            g_ref[2 * a + h] = total[8 * a : 8 * a + 8, 128 * h : 128 * h + 128]


def first_kernel(r_ref, d_ref, low_ref, high_ref, g_ref, kt_ref, j_ref, inf_ref, l_ref):
    inf_ref[...] = r_ref[pl.ds(4, 256, stride=5), :].T[:64]
    for r in range(4):
        block = r_ref[pl.ds(r, 256, stride=5), :].T
        for m in range(4):
            t = 4 * r + m
            kt_ref[:, 256 * t : 256 * t + 256] = block[32 * m : 32 * m + 32]
    row = iota((256, 256), 0).astype(F32)
    for t in range(16):
        hit = jnp.where(row == inf_ref[16 + t : 17 + t, :], 1.0, 0.0)
        j_ref[:, 256 * t : 256 * t + 256] = hit.astype(BF16)
    flat = scatter_rows(
        kt_ref, j_ref, inf_ref, l_ref, [inf_ref[48 + t : 49 + t, :] for t in range(16)]
    )
    cube = to_cube(flat)
    for i in range(8):
        d_ref[i] = cube[i]
    for i in range(2):
        low_ref[i] = cube[i]
        high_ref[i] = cube[6 + i]
    gather_rays(flat, kt_ref, j_ref, inf_ref, g_ref)


def lane_neighbours(x, axis):
    size = x.shape[axis]
    lane = lax.broadcasted_iota(I32, x.shape, axis)
    up = jnp.where(lane == 0, 0.0, pltpu.roll(x, 1, axis=axis))
    down = jnp.where(lane == size - 1, 0.0, pltpu.roll(x, size - 1, axis=axis))
    return up + down


def square_kernel(ev_ref, d_ref, low_ref, high_ref, before_ref, after_ref, out_ref, e_ref, f_ref):
    ev = ev_ref[0]
    has_low = jnp.where(ev > 0, 1.0, 0.0)
    has_high = jnp.where(ev < 3, 1.0, 0.0)
    for i in range(12):
        if i < 2:
            own = low_ref[i]
        elif i < 10:
            own = d_ref[i - 2]
        else:
            own = high_ref[i - 10]
        e_ref[i, 8:40] = own
    for i in range(1, 11):
        index = 9 if i == 1 else i - 2
        e_ref[i, 0:8] = before_ref[index, 24:32] * has_low
        e_ref[i, 40:48] = after_ref[index, 0:8] * has_high
    for i in (0, 11):
        e_ref[i, 0:8] = jnp.zeros((8, 128), F32)
        e_ref[i, 40:48] = jnp.zeros((8, 128), F32)
    radial = iota((48, 128), 0)
    inside = jnp.where(radial < 8, has_low, jnp.where(radial >= 40, has_high, 1.0))

    def laplace(ref, i):
        x = ref[i]
        radial_sum = pltpu.roll(x, 1, axis=0) + pltpu.roll(x, 47, axis=0)
        return 6.0 * x - (ref[i - 1] + ref[i + 1] + radial_sum + lane_neighbours(x, 1))

    for i in range(1, 11):
        f_ref[i] = laplace(e_ref, i) * inside
    for i in range(2, 10):
        out_ref[i - 2] = laplace(f_ref, i)[8:40]


def second_kernel(
    g0_ref, kt_ref, j_ref, inf_ref, d_ref, ll_ref,
    w_ref, low_ref, high_ref, g_ref, scal_ref, l_ref,
):
    rays = jnp.concatenate(
        [jnp.concatenate([g0_ref[2 * a], g0_ref[2 * a + 1]], axis=1) for a in range(4)], axis=0
    )
    ray_index = iota((32, 256), 0).astype(F32)
    weights = [
        jnp.sum(
            jnp.where(inf_ref[32 + t : 33 + t, :] == ray_index, rays, 0.0), axis=0, keepdims=True
        )
        for t in range(16)
    ]
    flat = scatter_rows(kt_ref, j_ref, inf_ref, l_ref, weights)
    cube = to_cube(flat)
    cube = [cube[i] + (damping * damping) * ll_ref[i] for i in range(8)]
    dd = jnp.zeros((32, 128), F32)
    dw = jnp.zeros((32, 128), F32)
    ww = jnp.zeros((32, 128), F32)
    for i in range(8):
        w_ref[i] = cube[i]
        d = d_ref[i]
        dd = dd + d * d
        dw = dw + d * cube[i]
        ww = ww + cube[i] * cube[i]
    low_ref[0] = cube[0]
    high_ref[0] = cube[7]
    scal_ref[0:1] = jnp.sum(dd, axis=0, keepdims=True)
    scal_ref[1:2] = jnp.sum(dw, axis=0, keepdims=True)
    scal_ref[2:3] = jnp.sum(ww, axis=0, keepdims=True)
    whole = jnp.concatenate(
        [jnp.concatenate([cube[2 * i], cube[2 * i + 1]], axis=1) for i in range(4)], axis=0
    )
    gather_rays(whole, kt_ref, j_ref, inf_ref, g_ref)


def norms_kernel(
    ev_ref, w_ref, low_ref, high_ref, before_ref, after_ref, scal_ref, delay_ref, part_ref,
    out_ref, e_ref,
):
    ev = ev_ref[0]
    has_low = jnp.where(ev > 0, 1.0, 0.0)
    has_high = jnp.where(ev < 3, 1.0, 0.0)
    square = jnp.zeros((32, 128), F32)
    for i in range(8):
        e_ref[8:40] = w_ref[i]
        e_ref[0:8] = before_ref[i, 24:32] * has_low
        e_ref[40:48] = after_ref[i, 0:8] * has_high
        x = w_ref[i]
        left = low_ref[0] if i == 0 else w_ref[i - 1]
        right = high_ref[0] if i == 7 else w_ref[i + 1]
        value = 6.0 * x - (
            left + right + e_ref[7:39] + e_ref[9:41] + lane_neighbours(x, 1)
        )
        square = square + value * value
    lane = iota((1, 128), 1)
    b = delay_ref[...]
    numbers = [
        jnp.sum(scal_ref[0:1], axis=1, keepdims=True),
        jnp.sum(scal_ref[1:2], axis=1, keepdims=True),
        jnp.sum(scal_ref[2:3], axis=1, keepdims=True),
        jnp.sum(b * b, axis=1, keepdims=True),
        jnp.sum(jnp.sum(square, axis=0, keepdims=True), axis=1, keepdims=True),
    ]
    row = jnp.zeros((1, 128), F32)
    for n, number in enumerate(numbers):
        row = jnp.where(lane == n, number, row)
    total = part_ref[0]
    for i in range(1, 8):
        total = total + part_ref[i]
    for p in range(32):
        out_ref[9 * p : 9 * p + 8] = total
        out_ref[9 * p + 8 : 9 * p + 9] = row


def ray_norm_kernel(x_ref, out_ref):
    total = x_ref[0:8]
    row = x_ref[8:9]
    for p in range(1, 32):
        total = total + x_ref[9 * p : 9 * p + 8]
        row = row + x_ref[9 * p + 8 : 9 * p + 9]
    norm = jnp.sum(jnp.sum(total * total, axis=0, keepdims=True), axis=1, keepdims=True)
    row = jnp.where(iota((1, 128), 1) == 5, norm, row)
    out_ref[...] = jnp.broadcast_to(row, (8, 128))


def final_kernel(
    ev_ref, scal_ref, d0_ref, d1_ref, d2_ref, d3_ref, w0_ref, w1_ref, w2_ref, w3_ref,
    out_ref, x_ref,
):
    sums = jnp.sum(scal_ref[...], axis=0, keepdims=True)
    lane = iota((1, 128), 1)

    def number(n):
        return jnp.sum(jnp.where(lane == n, sums, 0.0), axis=1, keepdims=True)

    dd, dw, ww, bb = number(0), number(1), number(2), number(3)
    aa = number(5) + (damping * damping) * number(4)
    eps = norm_epsilon
    beta0 = jnp.sqrt(bb + eps)
    alpha0 = jnp.sqrt(dd / (beta0 * beta0) + eps)
    sigma0 = 1.0 / (beta0 * alpha0)
    ratio0 = alpha0 / beta0
    square1 = sigma0 * sigma0 * dw - 2.0 * sigma0 * ratio0 * dd + ratio0 * ratio0 * bb
    beta1 = jnp.sqrt(jnp.maximum(square1, 0.0) + eps)
    rho1 = jnp.sqrt(alpha0 * alpha0 + beta1 * beta1)
    cosine1, sine1 = alpha0 / rho1, beta1 / rho1
    phi1 = cosine1 * beta0
    phi_bar1 = sine1 * beta0
    shift = alpha0 * alpha0 + beta1 * beta1
    error2 = jnp.maximum(ww - 2.0 * shift * dw + shift * shift * dd, 0.0)
    scale1 = sigma0 / beta1
    alpha1 = jnp.sqrt(scale1 * scale1 * error2 + eps)
    tau = scale1 / alpha1
    theta1 = sine1 * alpha1
    rho_bar1 = -cosine1 * alpha1
    c1 = tau
    c0 = -tau * shift - alpha1 * sigma0 / beta1
    cb = alpha1 * ratio0 / beta1
    square2 = (
        c1 * c1 * aa
        + 2.0 * c1 * c0 * ww
        + c0 * c0 * dw
        + cb * cb * bb
        + 2.0 * c1 * cb * dw
        + 2.0 * c0 * cb * dd
    )
    beta2 = jnp.sqrt(jnp.maximum(square2, 0.0) + eps)
    rho2 = jnp.sqrt(rho_bar1 * rho_bar1 + beta2 * beta2)
    cosine2 = rho_bar1 / rho2
    phi2 = cosine2 * phi_bar1
    step = phi2 / rho2
    k1 = step * tau
    k0 = phi1 / rho1 * sigma0 - step * (tau * shift + theta1 / rho1 * sigma0)
    ev = ev_ref[0]
    pairs = ((d0_ref, w0_ref), (d1_ref, w1_ref), (d2_ref, w2_ref), (d3_ref, w3_ref))
    for n, (d_ref, w_ref) in enumerate(pairs):
        owner = (ev - n) & 3
        for i in range(8):
            x_ref[i, pl.ds(pl.multiple_of(32 * owner, 32), 32), :] = k0 * d_ref[i] + k1 * w_ref[i]
    for i in range(8):
        out_ref[i] = x_ref[i].T


def exchange(x, axes):
    return lax.all_to_all(x, axes, split_axis=0, concat_axis=0, tiled=True)


def on_device(kernels, block_ids, delays):
    def ring(count, distance):
        return [(i, (i + distance) % count) for i in range(count)]

    def slab_shift(x, distance):
        return lax.ppermute(x, SLAB, ring(64, distance))

    def ev_shift(x, distance):
        return lax.ppermute(x, "ev", ring(4, distance))

    ev = lax.axis_index("ev").reshape(1)
    ev_spec = pl.BlockSpec(memory_space=pltpu.SMEM)

    def run_ev(body, args, out_shapes, scratch=()):
        outs = [jax.ShapeDtypeStruct(s, d) for s, d in out_shapes]
        return pl.pallas_call(
            body,
            out_shape=outs,
            in_specs=[ev_spec] + [VM] * len(args),
            out_specs=[VM] * len(outs),
            scratch_shapes=list(scratch),
            compiler_params=pltpu.CompilerParams(vmem_limit_bytes=40 << 20),
            cost_estimate=pl.CostEstimate(
                flops=1000000, bytes_accessed=1000000, transcendentals=0
            ),
        )(ev, *args)

    ids = block_ids.reshape(1, 1024)
    weights = jnp.repeat(delays, 32).reshape(1, 1024)
    (send,) = run(
        prep_kernel,
        (ids, weights, kernels.reshape(1024, 128)),
        [((1280, 128), F32)],
        [pltpu.VMEM((1024, 1024), BF16)],
    )
    received = exchange(send.reshape(256, 1, 640), ALL).reshape(1280, 128)

    cube = ((8, 32, 128), F32)
    d0, d_low, d_high, rays, kt, one_hot, info = run(
        first_kernel,
        (received,),
        [
            cube,
            ((2, 32, 128), F32),
            ((2, 32, 128), F32),
            ((8, 8, 128), F32),
            ((32, 4096), F32),
            ((256, 4096), BF16),
            ((64, 256), F32),
        ],
        [pltpu.VMEM((256, 4096), BF16)],
    )
    below = slab_shift(d_high, 1)
    above = slab_shift(d_low, -1)
    wide = jnp.concatenate([d0, above[:1], below[1:]], axis=0)
    d_1, d_2, d_3 = (ev_shift(wide, n) for n in (1, 2, 3))

    rays = exchange(rays, D1)
    rays = jnp.broadcast_to(jnp.sum(rays, axis=0)[None], (32, 8, 128))
    rays = exchange(rays, D2)
    rays = jnp.broadcast_to(jnp.sum(rays, axis=0)[None], (8, 8, 128))
    rays = exchange(rays, D1)

    (square,) = run_ev(
        square_kernel,
        (d0, below, above, d_1, d_3),
        [cube],
        [pltpu.VMEM((12, 48, 128), F32), pltpu.VMEM((12, 48, 128), F32)],
    )
    w1, w_low, w_high, rays1, scal = run(
        second_kernel,
        (rays, kt, one_hot, info, d0, square),
        [cube, ((1, 32, 128), F32), ((1, 32, 128), F32), ((8, 8, 128), F32), ((8, 128), F32)],
        [pltpu.VMEM((256, 4096), BF16)],
    )
    w_below = slab_shift(w_high, 1)
    w_above = slab_shift(w_low, -1)
    w_1, w_3, w_2 = (ev_shift(w1, n) for n in (1, 3, 2))
    rays1 = exchange(rays1, D1)
    (packed,) = run_ev(
        norms_kernel,
        (w1, w_below, w_above, w_1, w_3, scal, delays.reshape(1, 32), rays1),
        [((288, 128), F32)],
        [pltpu.VMEM((48, 128), F32)],
    )
    packed = exchange(packed.reshape(32, 1, 1152), D2).reshape(288, 128)
    (sums,) = run(ray_norm_kernel, (packed,), [((8, 128), F32)])
    sums = exchange(sums.reshape(8, 1, 128), D1).reshape(8, 128)
    (out,) = run_ev(
        final_kernel,
        (sums, d0, d_1, d_2, d_3, w1, w_1, w_2, w_3),
        [((8, 128, 128), F32)],
        [pltpu.VMEM((8, 128, 128), F32)],
    )
    return out


def solution(mesh):
    fine = Mesh(mesh.devices.reshape(4, 4, 8, 2), ALL)
    rays = P(ALL)
    return jax.shard_map(
        on_device, mesh=fine, in_specs=(rays, rays, rays), out_specs=P(SLAB), check_vma=False
    )
```

time: 1040 us -> 126 us (0.12)
  blocking collectives: 754 us -> 51 us
  waiting for transfers between devices: 121 us -> 24.9 us
  other arithmetic: 76.7 us -> 0.72 us
  local copies, waits for them, and re-layouts: 29.4 us -> 3.96 us
  between operations: 18.7 us -> 0.11 us
    psum x7 -> x0, blocking collectives: 731 us -> none  [the longest x2 255 us: finish_transpose(): lax.psum(jnp.sum(summed * summed), 'slab') + norm_epsilon]
    psum x2 -> x0, waiting for transfers between devices: 78.6 us -> none  [finish_transpose(): summed = lax.psum(partial_value, 'ev')]
    gather x4 -> x0, other arithmetic: 40.2 us -> none  [the longest x2 40.2 us: ray_transpose(): spread = ray_weights[ray_of]]
    all_to_all x1 -> x2, blocking collectives: 22.6 us -> 51 us  [exchange(): return lax.all_to_all(x, axes, split_axis=0, concat_axis=0, tiled=True)]
    gather x11 -> x0, local copies, waits for them, and re-layouts: 27.4 us -> none  [the longest x2 9.05 us: on_device(): entry_sums[position].reshape(ray_count, per_ray)]
    ppermute x6 -> x10, waiting for transfers between devices: 22.3 us -> 3.48 us  [the longest x4 3.46 us: slab_shift(): return lax.ppermute(x, SLAB, ring(64, distance))]
    scatter-add x2 -> x0, other arithmetic: 13.6 us -> none  [ray_transpose(): summed = jnp.zeros((cells_slab, width), jnp.float32).at[wanted].add(contrib)]
    all_to_all x4 -> x5, starting transfers between devices: 35.3 us -> 25.9 us  [exchange(): return lax.all_to_all(x, axes, split_axis=0, concat_axis=0, tiled=True)]
  transfers between devices with their start and end apart: 12 -> 15, of which waited for: 8 -> 7; matrix products, arithmetic and copies ran while one was open for 3% -> 2% of each run, Pallas kernels for 0% -> 1%
where the time goes in v1:
time: 126 us
  blocking collectives  51 us (40%)
  starting transfers between devices  34.8 us (28%)
  waiting for transfers between devices  24.9 us (20%)
  Pallas kernels  10.2 us (8%)
  local copies, waits for them, and re-layouts  3.96 us (3%)
    all_to_all x2, blocking collectives, exchange(): return lax.all_to_all(x, axes, split_axis=0, concat_axis=0, tiled=True)  51 us
    all_to_all x5, starting transfers between devices, exchange(): return lax.all_to_all(x, axes, split_axis=0, concat_axis=0, tiled=True)  25.9 us
    all_to_all x5, waiting for transfers between devices, exchange(): return lax.all_to_all(x, axes, split_axis=0, concat_axis=0, tiled=True)  21.5 us
    pallas_call x4, Pallas kernels, run(): pl.pallas_call(body, out_shape=outs, in_specs=[VM] * len(args), out_specs...  7.69 us
    ppermute x6, starting transfers between devices, ev_shift(): return lax.ppermute(x, 'ev', ring(4, distance))  7.01 us
    ppermute x4, waiting for transfers between devices, slab_shift(): return lax.ppermute(x, SLAB, ring(64, distance))  3.46 us
  transfers between devices with their start and end apart: 15, of which 7 were waited for; matrix products, arithmetic and copies ran while one was open for 2% of the time, Pallas kernels for 1%

profile of v1, /device:TPU:1, one launch (start us, length us, event | category | flops | bytes accessed | tf_op | source)
XLA Modules:
  0.0 125.7 jit_solution(1497045998590265816)
XLA Ops:
  0.0 0.8 reshape.33.ids_ref
  0.8 0.7 broadcast_in_dim.6
  1.6 1.0 copy-done
  2.6 1.4 %shard_map.37 = f32[1280,128]{1,0:T(8,128)S(1)} custom-call(s32[1,1024]{1,0:T(1,128)S(1)} %reshape.33.ids_ref, f32[1,1024]{1,0:T(1,128)S(1)} %reshape_reshape.3.b_ref, f32[1024,128]{1,0:T(8,128)S(1)} %bitcast.14), custom_call_target="tpu_custom_call" | custom-call | flops 1000000 | bytes 1000000 | tf_op jit(solution)/shard_map/pallas_call | solution.py:49
  4.0 39.5 %all_to_all.35 = f32[256,1,640]{2,1,0:T(1,128)S(1)} all-to-all(f32[256,1,640]{2,1,0:T(1,128)S(1)} %bitcast.12), channel_id=1, replica_groups=mesh['ev'=4,'sx'=4,'sz'=8,'sc'=2] {'ev','sx','sz','sc'}, dimensions={0} | all-to-all | bytes 1310720 | tf_op jit(solution)/shard_map/all_to_all | solution.py:375
  43.5 2.5 %shard_map.38 = (f32[8,32,128]{2,1,0:T(8,128)S(1)}, f32[2,32,128]{2,1,0:T(8,128)S(1)}, f32[2,32,128]{2,1,0:T(8,128)S(1)}, f32[8,8,128]{2,1,0:T(8,128)S(1)}, f32[...) custom-call(f32[1280,128]{1,0:T(8,128)S(1)} %bitcast.11), custom_call_target="tpu_custom_call" | custom-call | flops 1000000 | bytes 1000000 | tf_op jit(solution)/shard_map/pallas_call | solution.py:49
  46.1 0.9 collective-permute-start
  46.9 11.5 %all_to_all.36 = f32[8,8,128]{2,1,0:T(8,128)S(1)} all-to-all(f32[8,8,128]{2,1,0:T(8,128)S(1)} %get-tuple-element.17), channel_id=1, replica_groups=mesh['ev'=4,'sx'=4,'sz'=8,'sc'=2] {'sx','sc'}, dimensions={0} | all-to-all | bytes 65536 | tf_op jit(solution)/shard_map/all_to_all | solution.py:375
  58.5 0.7 broadcast_in_dim.7
  59.1 3.9 %all-to-all-start.2 = ((f32[32,8,128]{2,1,0:T(8,128)}), f32[32,8,128]{2,1,0:T(8,128)S(1)}, u32[]{:S(2)}, u32[]{:S(2)}) async-start(f32[32,8,128]{2,1,0:T(8,128)} %broadcast_in_dim.7), calls=%async_computation.2 | async-start | bytes 262144 | tf_op jit(solution)/shard_map/all_to_all | solution.py:375
  63.0 0.7 pad_maximum_fusion
  63.7 2.5 %collective-permute-start.3 = (f32[10,32,128]{2,1,0:T(8,128)}, f32[10,32,128]{2,1,0:T(8,128)S(1)}, u32[]{:S(2)}, u32[]{:S(2)}) collective-permute-start(f32[10,32,128]{2,1,0:T(8,128)} %pad_maximum_fusion), channel_id=1, source_target_pairs={{0,192},{64,0},{128,64},{192,128},{1,193},{65,1},{129,65},{193,129... | collective-permute-start | bytes 491528 | tf_op jit(solution)/shard_map/ppermute | solution.py:386
  66.2 5.9 %all-to-all-done.2 = f32[32,8,128]{2,1,0:T(8,128)S(1)} async-done(((f32[32,8,128]{2,1,0:T(8,128)}), f32[32,8,128]{2,1,0:T(8,128)S(1)}, u32[]{:S(2)}, u32[]{:S(2)}) %all-to-all-start.2) | async-done | bytes 131104 | tf_op jit(solution)/shard_map/all_to_all | solution.py:375
  72.2 0.6 broadcast_in_dim.8
  72.8 5.3 %all-to-all-start.3 = ((f32[8,8,128]{2,1,0:T(8,128)}), f32[8,8,128]{2,1,0:T(8,128)S(1)}, u32[]{:S(2)}, u32[]{:S(2)}) async-start(f32[8,8,128]{2,1,0:T(8,128)} %broadcast_in_dim.8), calls=%async_computation.3 | async-start | bytes 65536 | tf_op jit(solution)/shard_map/all_to_all | solution.py:375
  78.4 4.5 %all-to-all-done.3.g0_ref = f32[8,8,128]{2,1,0:T(8,128)S(1)} async-done(((f32[8,8,128]{2,1,0:T(8,128)}), f32[8,8,128]{2,1,0:T(8,128)S(1)}, u32[]{:S(2)}, u32[]{:S(2)}) %all-to-all-start.3) | async-done | bytes 32800 | tf_op jit(solution)/shard_map/all_to_all | solution.py:375
  82.8 3.1 %shard_map.40 = (f32[8,32,128]{2,1,0:T(8,128)S(1)}, f32[1,32,128]{2,1,0:T(8,128)S(1)}, f32[1,32,128]{2,1,0:T(8,128)S(1)}, f32[8,8,128]{2,1,0:T(8,128)}, f32[8,128]{1,0:T(8,128)S(1)}) custom-call(f32[8,8,128]{2,1,0:T(8,128)S(1)} %all-to-all-done.3.g0_ref, f32[32,4096]{1,0:T(8,128)S(1)} %get-tuple-element.18.kt_ref, ...), custom_call_target="tpu_custom_call" | custom-call | flops 1000000 | bytes 1000000 | tf_op jit(solution)/shard_map/pallas_call | solution.py:49
  85.9 0.8 collective-permute-start.7
  86.8 0.6 collective-permute-start.6
  87.4 4.5 %all-to-all-start.4 = ((f32[8,8,128]{2,1,0:T(8,128)}), f32[8,8,128]{2,1,0:T(8,128)S(1)}, u32[]{:S(2)}, u32[]{:S(2)}) async-start(f32[8,8,128]{2,1,0:T(8,128)} %get-tuple-element.28), calls=%async_computation.4 | async-start | bytes 65536 | tf_op jit(solution)/shard_map/all_to_all | solution.py:375
  91.9 1.0 collective-permute-start.4
  92.9 0.9 collective-permute-done.4.low_ref
  93.8 2.6 %collective-permute-done.5.high_ref = f32[1,32,128]{2,1,0:T(8,128)S(1)} collective-permute-done((f32[1,32,128]{2,1,0:T(8,128)S(1)}, f32[1,32,128]{2,1,0:T(8,128)S(1)}, u32[]{:S(2)}, u32[]{:S(2)}) %collective-permute-start.5) | collective-permute-done | bytes 16416 | tf_op jit(solution)/shard_map/ppermute | solution.py:383
  96.4 0.3 all-to-all-done.4.part_ref
  96.7 0.9 shard_map.41
  97.6 8.0 %all-to-all-start.5 = ((f32[32,1,1152]{2,1,0:T(1,128)}), f32[32,1,1152]{2,1,0:T(1,128)S(1)}, u32[]{:S(2)}, u32[]{:S(2)}) async-start(f32[32,1,1152]{2,1,0:T(1,128)} %bitcast.5), calls=%async_computation.5 | async-start | bytes 294912 | tf_op jit(solution)/shard_map/all_to_all | solution.py:375
  105.6 2.8 %collective-permute-start.8 = (f32[10,32,128]{2,1,0:T(8,128)}, f32[10,32,128]{2,1,0:T(8,128)S(1)}, u32[]{:S(2)}, u32[]{:S(2)}) collective-permute-start(f32[10,32,128]{2,1,0:T(8,128)} %pad_maximum_fusion), channel_id=1, source_target_pairs={{0,128},{64,192},{128,0},{192,64},{1,129},{65,193},{129,1},{193,65... | collective-permute-start | bytes 491528 | tf_op jit(solution)/shard_map/ppermute | solution.py:386
  108.7 6.2 %all-to-all-done.5 = f32[32,1,1152]{2,1,0:T(1,128)S(1)} async-done(((f32[32,1,1152]{2,1,0:T(1,128)}), f32[32,1,1152]{2,1,0:T(1,128)S(1)}, u32[]{:S(2)}, u32[]{:S(2)}) %all-to-all-start.5) | async-done | bytes 147488 | tf_op jit(solution)/shard_map/all_to_all | solution.py:375
  114.9 0.7 shard_map.42
  115.6 4.2 %all-to-all-start.6 = ((f32[8,1,128]{2,1,0:T(1,128)}), f32[8,1,128]{2,1,0:T(1,128)S(1)}, u32[]{:S(2)}, u32[]{:S(2)}) async-start(f32[8,1,128]{2,1,0:T(1,128)} %bitcast.8), calls=%async_computation.6 | async-start | bytes 8192 | tf_op jit(solution)/shard_map/all_to_all | solution.py:375
  119.8 4.6 %all-to-all-done.6 = f32[8,1,128]{2,1,0:T(1,128)S(1)} async-done(((f32[8,1,128]{2,1,0:T(1,128)}), f32[8,1,128]{2,1,0:T(1,128)S(1)}, u32[]{:S(2)}, u32[]{:S(2)}) %all-to-all-start.6) | async-done | bytes 4128 | tf_op jit(solution)/shard_map/all_to_all | solution.py:375
  124.4 1.3 %shard_map.43 = f32[8,128,128]{2,1,0:T(8,128)} custom-call(s32[1]{0:T(128)} %bitcast.ev_ref, f32[8,128]{1,0:T(8,128)S(1)} %bitcast.15, f32[8,32,128]{2,1,0:T(8,128)S(1)} %get-tuple-element.21.d_ref.d0_ref, f32[10,32,128]{2,1,0:T(8,128)S(1)} %collective-permute-done.2.before_ref.d1_ref, f32[10,32,128]{2,1,0:T(8,128)S(1)} %collective-permute-done.8.d2_ref, ...), custom_call_target="tpu_custom_call" | custom-call | flops 1000000 | bytes 1000000 | tf_op jit(solution)/shard_map/pallas_call | solution.py:393
  (21 shorter events, 0.7 us)
Async XLA Ops:
  1.6 1.0 copy-start
  46.1 16.9 %collective-permute-start = (f32[2,32,128]{2,1,0:T(8,128)S(1)}, f32[2,32,128]{2,1,0:T(8,128)S(1)}, u32[]{:S(2)}, u32[]{:S(2)}) collective-permute-start(f32[2,32,128]{2,1,0:T(8,128)S(1)} %get-tuple-element.22), channel_id=1, source_target_pairs={{0,1},{1,2},{2,3},{3,4},{4,5},{5,6},{6,7},{7,8},{8,9},{9,10},{10,1... | collective-permute-start | bytes 98312 | tf_op jit(solution)/shard_map/ppermute | solution.py:383
  46.9 16.1 %collective-permute-start.1 = (f32[2,32,128]{2,1,0:T(8,128)S(1)}, f32[2,32,128]{2,1,0:T(8,128)S(1)}, u32[]{:S(2)}, u32[]{:S(2)}) collective-permute-start(f32[2,32,128]{2,1,0:T(8,128)S(1)} %get-tuple-element.23), channel_id=1, source_target_pairs={{0,63},{1,0},{2,1},{3,2},{4,3},{5,4},{6,5},{7,6},{8,7},{9,8},{10,9... | collective-permute-start | bytes 98312 | tf_op jit(solution)/shard_map/ppermute | solution.py:383
  59.1 13.0 %all-to-all-start.2 = ((f32[32,8,128]{2,1,0:T(8,128)}), f32[32,8,128]{2,1,0:T(8,128)S(1)}, u32[]{:S(2)}, u32[]{:S(2)}) async-start(f32[32,8,128]{2,1,0:T(8,128)} %broadcast_in_dim.7), calls=%async_computation.2 | async-start | bytes 262144 | tf_op jit(solution)/shard_map/all_to_all | solution.py:375
  63.0 33.6 %copy-start.1 = (f32[32]{0:T(128)S(1)}, f32[32]{0:T(128)}, u32[]{:S(2)}) copy-start(f32[32]{0:T(128)} %param.5) | copy-start | bytes 388
  63.7 14.4 %collective-permute-start.3 = (f32[10,32,128]{2,1,0:T(8,128)}, f32[10,32,128]{2,1,0:T(8,128)S(1)}, u32[]{:S(2)}, u32[]{:S(2)}) collective-permute-start(f32[10,32,128]{2,1,0:T(8,128)} %pad_maximum_fusion), channel_id=1, source_target_pairs={{0,192},{64,0},{128,64},{192,128},{1,193},{65,1},{129,65},{193,129... | collective-permute-start | bytes 491528 | tf_op jit(solution)/shard_map/ppermute | solution.py:386
  66.2 11.9 %collective-permute-start.2 = (f32[10,32,128]{2,1,0:T(8,128)}, f32[10,32,128]{2,1,0:T(8,128)S(1)}, u32[]{:S(2)}, u32[]{:S(2)}) collective-permute-start(f32[10,32,128]{2,1,0:T(8,128)} %pad_maximum_fusion), channel_id=1, source_target_pairs={{0,64},{64,128},{128,192},{192,0},{1,65},{65,129},{129,193},{193,1... | collective-permute-start | bytes 491528 | tf_op jit(solution)/shard_map/ppermute | solution.py:386
  72.8 10.0 %all-to-all-start.3 = ((f32[8,8,128]{2,1,0:T(8,128)}), f32[8,8,128]{2,1,0:T(8,128)S(1)}, u32[]{:S(2)}, u32[]{:S(2)}) async-start(f32[8,8,128]{2,1,0:T(8,128)} %broadcast_in_dim.8), calls=%async_computation.3 | async-start | bytes 65536 | tf_op jit(solution)/shard_map/all_to_all | solution.py:375
  85.9 10.7 %collective-permute-start.7 = (f32[8,32,128]{2,1,0:T(8,128)S(1)}, f32[8,32,128]{2,1,0:T(8,128)S(1)}, u32[]{:S(2)}, u32[]{:S(2)}) collective-permute-start(f32[8,32,128]{2,1,0:T(8,128)S(1)} %get-tuple-element.24.w_ref.w0_ref), channel_id=1, source_target_pairs={{0,192},{64,0},{128,64},{192,128},{1,193},{65,1},{129,65},{193,129... | collective-permute-start | bytes 393224 | tf_op jit(solution)/shard_map/ppermute | solution.py:386
  86.8 9.9 %collective-permute-start.6 = (f32[8,32,128]{2,1,0:T(8,128)S(1)}, f32[8,32,128]{2,1,0:T(8,128)S(1)}, u32[]{:S(2)}, u32[]{:S(2)}) collective-permute-start(f32[8,32,128]{2,1,0:T(8,128)S(1)} %get-tuple-element.24.w_ref.w0_ref), channel_id=1, source_target_pairs={{0,64},{64,128},{128,192},{192,0},{1,65},{65,129},{129,193},{193,1... | collective-permute-start | bytes 393224 | tf_op jit(solution)/shard_map/ppermute | solution.py:386
  87.4 9.3 %all-to-all-start.4 = ((f32[8,8,128]{2,1,0:T(8,128)}), f32[8,8,128]{2,1,0:T(8,128)S(1)}, u32[]{:S(2)}, u32[]{:S(2)}) async-start(f32[8,8,128]{2,1,0:T(8,128)} %get-tuple-element.28), calls=%async_computation.4 | async-start | bytes 65536 | tf_op jit(solution)/shard_map/all_to_all | solution.py:375
  91.9 1.9 %collective-permute-start.4 = (f32[1,32,128]{2,1,0:T(8,128)S(1)}, f32[1,32,128]{2,1,0:T(8,128)S(1)}, u32[]{:S(2)}, u32[]{:S(2)}) collective-permute-start(f32[1,32,128]{2,1,0:T(8,128)S(1)} %get-tuple-element.25), channel_id=1, source_target_pairs={{0,1},{1,2},{2,3},{3,4},{4,5},{5,6},{6,7},{7,8},{8,9},{9,10},{10,1... | collective-permute-start | bytes 49160 | tf_op jit(solution)/shard_map/ppermute | solution.py:383
  92.9 3.5 %collective-permute-start.5 = (f32[1,32,128]{2,1,0:T(8,128)S(1)}, f32[1,32,128]{2,1,0:T(8,128)S(1)}, u32[]{:S(2)}, u32[]{:S(2)}) collective-permute-start(f32[1,32,128]{2,1,0:T(8,128)S(1)} %get-tuple-element.26), channel_id=1, source_target_pairs={{0,63},{1,0},{2,1},{3,2},{4,3},{5,4},{6,5},{7,6},{8,7},{9,8},{10,9... | collective-permute-start | bytes 49160 | tf_op jit(solution)/shard_map/ppermute | solution.py:383
  97.6 17.3 %all-to-all-start.5 = ((f32[32,1,1152]{2,1,0:T(1,128)}), f32[32,1,1152]{2,1,0:T(1,128)S(1)}, u32[]{:S(2)}, u32[]{:S(2)}) async-start(f32[32,1,1152]{2,1,0:T(1,128)} %bitcast.5), calls=%async_computation.5 | async-start | bytes 294912 | tf_op jit(solution)/shard_map/all_to_all | solution.py:375
  105.6 14.2 %collective-permute-start.8 = (f32[10,32,128]{2,1,0:T(8,128)}, f32[10,32,128]{2,1,0:T(8,128)S(1)}, u32[]{:S(2)}, u32[]{:S(2)}) collective-permute-start(f32[10,32,128]{2,1,0:T(8,128)} %pad_maximum_fusion), channel_id=1, source_target_pairs={{0,128},{64,192},{128,0},{192,64},{1,129},{65,193},{129,1},{193,65... | collective-permute-start | bytes 491528 | tf_op jit(solution)/shard_map/ppermute | solution.py:386
  108.4 11.4 %collective-permute-start.9 = (f32[8,32,128]{2,1,0:T(8,128)S(1)}, f32[8,32,128]{2,1,0:T(8,128)S(1)}, u32[]{:S(2)}, u32[]{:S(2)}) collective-permute-start(f32[8,32,128]{2,1,0:T(8,128)S(1)} %get-tuple-element.24.w_ref.w0_ref), channel_id=1, source_target_pairs={{0,128},{64,192},{128,0},{192,64},{1,129},{65,193},{129,1},{193,65... | collective-permute-start | bytes 393224 | tf_op jit(solution)/shard_map/ppermute | solution.py:386
  115.6 8.8 %all-to-all-start.6 = ((f32[8,1,128]{2,1,0:T(1,128)}), f32[8,1,128]{2,1,0:T(1,128)S(1)}, u32[]{:S(2)}, u32[]{:S(2)}) async-start(f32[8,1,128]{2,1,0:T(1,128)} %bitcast.8), calls=%async_computation.6 | async-start | bytes 8192 | tf_op jit(solution)/shard_map/all_to_all | solution.py:375

commit v2 on v1

--- a/solution.py
+++ b/solution.py
@@ -5,8 +5,6 @@
 from jax.experimental.pallas import tpu as pltpu
 from jax.sharding import Mesh, PartitionSpec as P
 
-CX = 8
-NY = 128
 damping = 0.3
 norm_epsilon = 1e-06
 
@@ -18,6 +16,8 @@
 SLAB = ("sx", "sz", "sc")
 D1 = ("sx", "sc")
 D2 = ("ev", "sz")
+NEAR = ("ev", "sc")
+FAR = ("sx", "sz")
 
 VM = pl.BlockSpec(memory_space=pltpu.VMEM)
 
@@ -29,19 +29,6 @@
 def split2(x):
     hi = x.astype(BF16)
     return hi, (x - hi.astype(F32)).astype(BF16)
-
-
-def call(body, out_shapes, scratch=(), flops=1000000, nbytes=1000000):
-    outs = [jax.ShapeDtypeStruct(s, d) for s, d in out_shapes]
-    return pl.pallas_call(
-        body,
-        out_shape=outs,
-        in_specs=None,
-        out_specs=[VM] * len(outs),
-        scratch_shapes=list(scratch),
-        compiler_params=pltpu.CompilerParams(vmem_limit_bytes=40 << 20),
-        cost_estimate=pl.CostEstimate(flops=flops, bytes_accessed=nbytes, transcendentals=0),
-    )
 
 
 def run(body, args, out_shapes, scratch=(), flops=1000000, nbytes=1000000):
@@ -52,13 +39,36 @@
         in_specs=[VM] * len(args),
         out_specs=[VM] * len(outs),
         scratch_shapes=list(scratch),
-        compiler_params=pltpu.CompilerParams(vmem_limit_bytes=40 << 20),
+        compiler_params=pltpu.CompilerParams(vmem_limit_bytes=16 << 20),
         cost_estimate=pl.CostEstimate(flops=flops, bytes_accessed=nbytes, transcendentals=0),
     )(*args)
 
 
-def prep_kernel(ids_ref, b_ref, k_ref, send_ref, oh_ref):
-    ids = ids_ref[...]
+def prep_kernel(ids_hbm, b_hbm, k_hbm, send_ref, oh_ref, ids_ref, b_ref, k_ref, sem):
+    ids_copy = pltpu.make_async_copy(ids_hbm, ids_ref, sem.at[0])
+    b_copy = pltpu.make_async_copy(b_hbm, b_ref, sem.at[1])
+    copy = pltpu.make_async_copy(k_hbm, k_ref, sem.at[2])
+    ids_copy.start()
+    b_copy.start()
+    copy.start()
+    entry = iota((32, 1024), 1)
+    sub = iota((32, 1024), 0)
+    spread_k = jnp.where((entry & 31) == sub, 1.0, 0.0).astype(BF16)
+    spread_ray = jnp.where(lax.shift_right_logical(entry, 5) == sub, 1.0, 0.0)
+    ids_copy.wait()
+    b_copy.wait()
+    ids2 = ids_ref[...]
+    halves = jnp.concatenate(
+        [lax.shift_right_logical(ids2, 8).astype(F32), (ids2 & 255).astype(F32)], axis=0
+    )
+    halves = jnp.dot(halves.astype(BF16), spread_k, preferred_element_type=F32)
+    ids = jnp.sum((halves[:32] * 256.0 + halves[32:]) * spread_ray, axis=0, keepdims=True)
+    ids = ids.astype(I32)
+    b = b_ref[...]
+    b_hi = b.astype(BF16)
+    b_mid, b_lo = split2(b - b_hi.astype(F32))
+    b_rows = jnp.concatenate([jnp.broadcast_to(v, (16, 32)) for v in (b_hi, b_mid, b_lo)], axis=0)
+    b_rows = jnp.dot(b_rows, spread_ray.astype(BF16), preferred_element_type=F32).astype(BF16)
     slab = lax.shift_right_logical(ids, 10)
     loc = ids & 1023
     s_f = (iota((64, 1024), 0) == slab).astype(F32)
@@ -82,6 +92,7 @@
         for r in range(4):
             pick = jnp.where(rank == float(4 * r + m), 1.0, 0.0).astype(BF16)
             oh_ref[64 * (4 * m + r) : 64 * (4 * m + r) + 64, :] = s_b * pick
+    copy.wait()
     k_hi, k_lo = split2(k_ref[...])
     both = jnp.dot(
         oh_ref[...], jnp.concatenate([k_hi, k_lo], axis=1), preferred_element_type=F32
@@ -101,11 +112,8 @@
     group = lax.shift_right_logical(loc_i, 1).astype(F32)
     column = ((loc_i & 1) * 128 + (loc & 127)).astype(F32)
     ray = lax.shift_right_logical(iota((1, 1024), 1), 5).astype(F32)
-    b = b_ref[...]
-    b_hi, rest = b.astype(BF16), None
-    rest = b - b_hi.astype(F32)
-    b_mid, b_lo = split2(rest)
-    values = [group.astype(BF16), column.astype(BF16), ray.astype(BF16), b_hi, b_mid, b_lo]
+    b_parts = [b_rows[16 * i : 16 * i + 1] for i in range(3)]
+    values = [group.astype(BF16), column.astype(BF16), ray.astype(BF16)] + b_parts
     left = jnp.concatenate([s_b * v for v in values], axis=0)
     slot = (iota((128, 1024), 0) & 15).astype(F32)
     right = jnp.where(slot == rank, 1.0, 0.0).astype(BF16)
@@ -159,7 +167,7 @@
         total = total + jnp.where(inf_ref[32 + t : 33 + t, :] == ray_index, entry, 0.0)
     for a in range(4):
         for h in range(2):
-            g_ref[2 * a + h] = total[8 * a : 8 * a + 8, 128 * h : 128 * h + 128]
+            g_ref[2 * a + h, 0:8] = total[8 * a : 8 * a + 8, 128 * h : 128 * h + 128]
 
 
 def first_kernel(r_ref, d_ref, low_ref, high_ref, g_ref, kt_ref, j_ref, inf_ref, l_ref):
@@ -193,8 +201,7 @@
     return up + down
 
 
-def square_kernel(ev_ref, d_ref, low_ref, high_ref, before_ref, after_ref, out_ref, e_ref, f_ref):
-    ev = ev_ref[0]
+def apply_square(ev, d_ref, low_ref, high_ref, before_ref, after_ref, e_ref, f_ref):
     has_low = jnp.where(ev > 0, 1.0, 0.0)
     has_high = jnp.where(ev < 3, 1.0, 0.0)
     for i in range(12):
@@ -222,14 +229,15 @@
 
     for i in range(1, 11):
         f_ref[i] = laplace(e_ref, i) * inside
-    for i in range(2, 10):
-        out_ref[i - 2] = laplace(f_ref, i)[8:40]
+    return [laplace(f_ref, i)[8:40] for i in range(2, 10)]
 
 
 def second_kernel(
-    g0_ref, kt_ref, j_ref, inf_ref, d_ref, ll_ref,
-    w_ref, low_ref, high_ref, g_ref, scal_ref, l_ref,
+    place_ref, g0_ref, kt_ref, j_ref, inf_ref, d_ref, below_ref, above_ref, before_ref, after_ref,
+    w_ref, edge_ref, near_ref, g_ref, scal_ref, l_ref, e_ref, f_ref,
 ):
+    ev = lax.shift_right_logical(place_ref[0], 6)
+    core = place_ref[0] & 1
     rays = jnp.concatenate(
         [jnp.concatenate([g0_ref[2 * a], g0_ref[2 * a + 1]], axis=1) for a in range(4)], axis=0
     )
@@ -242,7 +250,8 @@
     ]
     flat = scatter_rows(kt_ref, j_ref, inf_ref, l_ref, weights)
     cube = to_cube(flat)
-    cube = [cube[i] + (damping * damping) * ll_ref[i] for i in range(8)]
+    square = apply_square(ev, d_ref, below_ref, above_ref, before_ref, after_ref, e_ref, f_ref)
+    cube = [cube[i] + (damping * damping) * square[i] for i in range(8)]
     dd = jnp.zeros((32, 128), F32)
     dw = jnp.zeros((32, 128), F32)
     ww = jnp.zeros((32, 128), F32)
@@ -252,8 +261,13 @@
         dd = dd + d * d
         dw = dw + d * cube[i]
         ww = ww + cube[i] * cube[i]
-    low_ref[0] = cube[0]
-    high_ref[0] = cube[7]
+    even = jnp.where(core == 0, 1.0, 0.0)
+    edge_ref[0] = even * cube[0] + (1.0 - even) * cube[7]
+    near_ref[0] = even * cube[7] + (1.0 - even) * cube[0]
+    first = jnp.concatenate([cube[i][0:1] for i in range(8)], axis=0)
+    last = jnp.concatenate([cube[i][31:32] for i in range(8)], axis=0)
+    g_ref[2 * ((ev + 1) & 3) + core, 8:16] = last
+    g_ref[2 * ((ev + 3) & 3) + core, 8:16] = first
     scal_ref[0:1] = jnp.sum(dd, axis=0, keepdims=True)
     scal_ref[1:2] = jnp.sum(dw, axis=0, keepdims=True)
     scal_ref[2:3] = jnp.sum(ww, axis=0, keepdims=True)
@@ -263,21 +277,26 @@
     gather_rays(whole, kt_ref, j_ref, inf_ref, g_ref)
 
 
-def norms_kernel(
-    ev_ref, w_ref, low_ref, high_ref, before_ref, after_ref, scal_ref, delay_ref, part_ref,
-    out_ref, e_ref,
-):
-    ev = ev_ref[0]
+def norms_kernel(place_ref, w_ref, edge_ref, near_ref, scal_ref, delay_ref, part_ref, out_ref, e_ref):
+    ev = lax.shift_right_logical(place_ref[0], 6)
+    core = place_ref[0] & 1
+    even = jnp.where(core == 0, 1.0, 0.0)
     has_low = jnp.where(ev > 0, 1.0, 0.0)
     has_high = jnp.where(ev < 3, 1.0, 0.0)
+    partner = near_ref[0]
+    far = edge_ref[0]
+    low = even * far + (1.0 - even) * partner
+    high = even * partner + (1.0 - even) * far
+    before = part_ref[2 * ((ev + 3) & 3) + core, 8:16] * has_low
+    after = part_ref[2 * ((ev + 1) & 3) + core, 8:16] * has_high
     square = jnp.zeros((32, 128), F32)
     for i in range(8):
-        e_ref[8:40] = w_ref[i]
-        e_ref[0:8] = before_ref[i, 24:32] * has_low
-        e_ref[40:48] = after_ref[i, 0:8] * has_high
         x = w_ref[i]
-        left = low_ref[0] if i == 0 else w_ref[i - 1]
-        right = high_ref[0] if i == 7 else w_ref[i + 1]
+        e_ref[8:40] = x
+        e_ref[7:8] = before[i : i + 1]
+        e_ref[40:41] = after[i : i + 1]
+        left = low if i == 0 else w_ref[i - 1]
+        right = high if i == 7 else w_ref[i + 1]
         value = 6.0 * x - (
             left + right + e_ref[7:39] + e_ref[9:41] + lane_neighbours(x, 1)
         )
@@ -294,12 +313,20 @@
     row = jnp.zeros((1, 128), F32)
     for n, number in enumerate(numbers):
         row = jnp.where(lane == n, number, row)
-    total = part_ref[0]
+    total = part_ref[0, 0:8]
     for i in range(1, 8):
-        total = total + part_ref[i]
+        total = total + part_ref[i, 0:8]
     for p in range(32):
         out_ref[9 * p : 9 * p + 8] = total
         out_ref[9 * p + 8 : 9 * p + 9] = row
+
+
+def spread_kernel(x_ref, out_ref):
+    total = x_ref[0]
+    for i in range(1, x_ref.shape[0]):
+        total = total + x_ref[i]
+    for i in range(out_ref.shape[0]):
+        out_ref[i] = total
 
 
 def ray_norm_kernel(x_ref, out_ref):
@@ -314,7 +341,7 @@
 
 
 def final_kernel(
-    ev_ref, scal_ref, d0_ref, d1_ref, d2_ref, d3_ref, w0_ref, w1_ref, w2_ref, w3_ref,
+    place_ref, scal_ref, d0_ref, d1_ref, d2_ref, d3_ref, w0_ref, w1_ref, w2_ref, w3_ref,
     out_ref, x_ref,
 ):
     sums = jnp.sum(scal_ref[...], axis=0, keepdims=True)
@@ -361,7 +388,7 @@
     step = phi2 / rho2
     k1 = step * tau
     k0 = phi1 / rho1 * sigma0 - step * (tau * shift + theta1 / rho1 * sigma0)
-    ev = ev_ref[0]
+    ev = lax.shift_right_logical(place_ref[0], 6)
     pairs = ((d0_ref, w0_ref), (d1_ref, w1_ref), (d2_ref, w2_ref), (d3_ref, w3_ref))
     for n, (d_ref, w_ref) in enumerate(pairs):
         owner = (ev - n) & 3
@@ -375,7 +402,7 @@
     return lax.all_to_all(x, axes, split_axis=0, concat_axis=0, tiled=True)
 
 
-def on_device(kernels, block_ids, delays):
+def body(kernels, block_ids, delays):
     def ring(count, distance):
         return [(i, (i + distance) % count) for i in range(count)]
 
@@ -385,7 +412,7 @@
     def ev_shift(x, distance):
         return lax.ppermute(x, "ev", ring(4, distance))
 
-    ev = lax.axis_index("ev").reshape(1)
+    place = lax.axis_index(ALL).reshape(1)
     ev_spec = pl.BlockSpec(memory_space=pltpu.SMEM)
 
     def run_ev(body, args, out_shapes, scratch=()):
@@ -396,20 +423,26 @@
             in_specs=[ev_spec] + [VM] * len(args),
             out_specs=[VM] * len(outs),
             scratch_shapes=list(scratch),
-            compiler_params=pltpu.CompilerParams(vmem_limit_bytes=40 << 20),
+            compiler_params=pltpu.CompilerParams(vmem_limit_bytes=16 << 20),
             cost_estimate=pl.CostEstimate(
                 flops=1000000, bytes_accessed=1000000, transcendentals=0
             ),
-        )(ev, *args)
-
-    ids = block_ids.reshape(1, 1024)
-    weights = jnp.repeat(delays, 32).reshape(1, 1024)
-    (send,) = run(
+        )(place, *args)
+
+    send = pl.pallas_call(
         prep_kernel,
-        (ids, weights, kernels.reshape(1024, 128)),
-        [((1280, 128), F32)],
-        [pltpu.VMEM((1024, 1024), BF16)],
-    )
+        out_shape=jax.ShapeDtypeStruct((1280, 128), F32),
+        in_specs=[pl.BlockSpec(memory_space=pltpu.MemorySpace.HBM)] * 3,
+        out_specs=VM,
+        scratch_shapes=[
+            pltpu.VMEM((1024, 1024), BF16),
+            pltpu.VMEM((32, 32), I32),
+            pltpu.VMEM((1, 32), F32),
+            pltpu.VMEM((1024, 128), F32),
+            pltpu.SemaphoreType.DMA((3,)),
+        ],
+        compiler_params=pltpu.CompilerParams(vmem_limit_bytes=63 << 20),
+    )(block_ids, delays.reshape(1, 32), kernels.reshape(1024, 128))
     received = exchange(send.reshape(256, 1, 640), ALL).reshape(1280, 128)
 
     cube = ((8, 32, 128), F32)
@@ -433,36 +466,36 @@
     d_1, d_2, d_3 = (ev_shift(wide, n) for n in (1, 2, 3))
 
     rays = exchange(rays, D1)
-    rays = jnp.broadcast_to(jnp.sum(rays, axis=0)[None], (32, 8, 128))
+    (rays,) = run(spread_kernel, (rays,), [((32, 8, 128), F32)])
     rays = exchange(rays, D2)
-    rays = jnp.broadcast_to(jnp.sum(rays, axis=0)[None], (8, 8, 128))
+    (rays,) = run(spread_kernel, (rays,), [((8, 8, 128), F32)])
     rays = exchange(rays, D1)
 
-    (square,) = run_ev(
-        square_kernel,
-        (d0, below, above, d_1, d_3),
-        [cube],
-        [pltpu.VMEM((12, 48, 128), F32), pltpu.VMEM((12, 48, 128), F32)],
-    )
-    w1, w_low, w_high, rays1, scal = run(
+    w1, w_edge, w_near, rays1, scal = run_ev(
         second_kernel,
-        (rays, kt, one_hot, info, d0, square),
-        [cube, ((1, 32, 128), F32), ((1, 32, 128), F32), ((8, 8, 128), F32), ((8, 128), F32)],
-        [pltpu.VMEM((256, 4096), BF16)],
-    )
-    w_below = slab_shift(w_high, 1)
-    w_above = slab_shift(w_low, -1)
-    w_1, w_3, w_2 = (ev_shift(w1, n) for n in (1, 3, 2))
-    rays1 = exchange(rays1, D1)
+        (rays, kt, one_hot, info, d0, below, above, d_1, d_3),
+        [cube, ((1, 32, 128), F32), ((1, 32, 128), F32), ((8, 16, 128), F32), ((8, 128), F32)],
+        [
+            pltpu.VMEM((256, 4096), BF16),
+            pltpu.VMEM((12, 48, 128), F32),
+            pltpu.VMEM((12, 48, 128), F32),
+        ],
+    )
+    pairs = [(i, (i + 1) % 64 if i % 2 else (i - 1) % 64) for i in range(64)]
+    w_far = lax.ppermute(w_edge, SLAB, pairs)
+    w_near = lax.ppermute(w_near, "sc", [(0, 1), (1, 0)])
+    rays1 = exchange(rays1, NEAR)
     (packed,) = run_ev(
         norms_kernel,
-        (w1, w_below, w_above, w_1, w_3, scal, delays.reshape(1, 32), rays1),
+        (w1, w_far, w_near, scal, delays.reshape(1, 32), rays1),
         [((288, 128), F32)],
         [pltpu.VMEM((48, 128), F32)],
     )
-    packed = exchange(packed.reshape(32, 1, 1152), D2).reshape(288, 128)
+    w_1, w_2, w_3 = (ev_shift(w1, n) for n in (1, 2, 3))
+    packed = exchange(packed.reshape(32, 1, 1152), FAR).reshape(288, 128)
+    packed, d_2, w_1, w_2, w_3 = lax.optimization_barrier((packed, d_2, w_1, w_2, w_3))
     (sums,) = run(ray_norm_kernel, (packed,), [((8, 128), F32)])
-    sums = exchange(sums.reshape(8, 1, 128), D1).reshape(8, 128)
+    sums = exchange(sums.reshape(8, 1, 128), NEAR).reshape(8, 128)
     (out,) = run_ev(
         final_kernel,
         (sums, d0, d_1, d_2, d_3, w1, w_1, w_2, w_3),
@@ -476,5 +509,5 @@
     fine = Mesh(mesh.devices.reshape(4, 4, 8, 2), ALL)
     rays = P(ALL)
     return jax.shard_map(
-        on_device, mesh=fine, in_specs=(rays, rays, rays), out_specs=P(SLAB), check_vma=False
-    )
+        body, mesh=fine, in_specs=(rays, rays, rays), out_specs=P(SLAB), check_vma=False
+    )

time: 126 us -> 124 us (0.984)
  blocking collectives: 51 us -> 62.5 us
  starting transfers between devices: 34.8 us -> 26.6 us
  local copies, waits for them, and re-layouts: 3.96 us -> 0.02 us
  waiting for transfers between devices: 24.9 us -> 21.7 us
  Pallas kernels: 10.2 us -> 12.6 us
    all_to_all x2 -> x3, blocking collectives: 51 us -> 62.5 us  [exchange(): return lax.all_to_all(x, axes, split_axis=0, concat_axis=0, tiled=True)]
    all_to_all x5 -> x4, waiting for transfers between devices: 21.5 us -> 12.7 us  [exchange(): return lax.all_to_all(x, axes, split_axis=0, concat_axis=0, tiled=True)]
    all_to_all x5 -> x4, starting transfers between devices: 25.9 us -> 17.1 us  [exchange(): return lax.all_to_all(x, axes, split_axis=0, concat_axis=0, tiled=True)]
    ppermute x6, waiting for transfers between devices: 0.02 us -> 6.6 us  [ev_shift(): return lax.ppermute(x, 'ev', ring(4, distance))]
    pallas_call x4, Pallas kernels: 7.69 us -> 3.96 us  [run(): pl.pallas_call(body, out_shape=outs, in_specs=[VM] * len(args), out_specs...]
    ppermute x4 -> x2, waiting for transfers between devices: 3.46 us -> 0.01 us  [slab_shift(): return lax.ppermute(x, SLAB, ring(64, distance))]
    pallas_call x0 -> x1, Pallas kernels: none -> 3.26 us  [body(): pl.pallas_call(prep_kernel, out_shape=jax.ShapeDtypeStruct((1280, 128), F...]
    pallas_call x3, Pallas kernels: 2.5 us -> 5.35 us  [run_ev(): pl.pallas_call(body, out_shape=outs, in_specs=[ev_spec] + [VM] * len(args...]
  transfers between devices with their start and end apart: 15 -> 14, of which waited for: 7 -> 8; matrix products, arithmetic and copies ran while one was open for 2% -> 0% of each run, Pallas kernels for 1% -> 1%
where the time goes in v2:
time: 124 us
  blocking collectives  62.5 us (50%)
  starting transfers between devices  26.6 us (21%)
  waiting for transfers between devices  21.7 us (18%)
  Pallas kernels  12.6 us (10%)
    all_to_all x3, blocking collectives, exchange(): return lax.all_to_all(x, axes, split_axis=0, concat_axis=0, tiled=True)  62.5 us
    all_to_all x4, starting transfers between devices, exchange(): return lax.all_to_all(x, axes, split_axis=0, concat_axis=0, tiled=True)  17.1 us
    all_to_all x4, waiting for transfers between devices, exchange(): return lax.all_to_all(x, axes, split_axis=0, concat_axis=0, tiled=True)  12.7 us
    ppermute x6, starting transfers between devices, ev_shift(): return lax.ppermute(x, 'ev', ring(4, distance))  7.58 us
    ppermute x6, waiting for transfers between devices, ev_shift(): return lax.ppermute(x, 'ev', ring(4, distance))  6.6 us
    pallas_call x3, Pallas kernels, run_ev(): pl.pallas_call(body, out_shape=outs, in_specs=[ev_spec] + [VM] * len(args...  5.35 us
    pallas_call x4, Pallas kernels, run(): pl.pallas_call(body, out_shape=outs, in_specs=[VM] * len(args), out_specs...  3.96 us
    pallas_call x1, Pallas kernels, body(): pl.pallas_call(prep_kernel, out_shape=jax.ShapeDtypeStruct((1280, 128), F...  3.26 us
  transfers between devices with their start and end apart: 14, of which 8 were waited for; matrix products, arithmetic and copies ran while one was open for 0% of the time, Pallas kernels for 1%

profile of v2, /device:TPU:1, one launch (start us, length us, event | category | flops | bytes accessed | tf_op | source)
XLA Modules:
  0.0 123.5 jit_solution(641647873201436330)
XLA Ops:
  0.0 3.3 %shard_map.37 = f32[1280,128]{1,0:T(8,128)} custom-call(s32[32,32]{1,0:T(8,128)} %ids_hbm.1, f32[1,32]{1,0:T(1,128)} %bitcast.15, f32[1024,128]{1,0:T(8,128)} %bitcast.18), custom_call_target="tpu_custom_call" | custom-call | tf_op jit(solution)/shard_map/pallas_call | solution.py:432
  3.3 39.7 %all_to_all.35 = f32[256,1,640]{2,1,0:T(1,128)S(1)} all-to-all(f32[256,1,640]{2,1,0:T(1,128)} %bitcast.17), channel_id=1, replica_groups=mesh['ev'=4,'sx'=4,'sz'=8,'sc'=2] {'ev','sx','sz','sc'}, dimensions={0} | all-to-all | bytes 1310720 | tf_op jit(solution)/shard_map/all_to_all | solution.py:402
  43.0 2.5 %shard_map.38 = (f32[8,32,128]{2,1,0:T(8,128)S(1)}, f32[2,32,128]{2,1,0:T(8,128)S(1)}, f32[2,32,128]{2,1,0:T(8,128)S(1)}, f32[8,8,128]{2,1,0:T(8,128)S(1)}, f32[...) custom-call(f32[1280,128]{1,0:T(8,128)S(1)} %bitcast.11), custom_call_target="tpu_custom_call" | custom-call | flops 1000000 | bytes 1000000 | tf_op jit(solution)/shard_map/pallas_call | solution.py:36
  45.5 0.9 collective-permute-start
  46.4 0.0 collective-permute-start.1
  46.4 11.5 %all_to_all.36.x_ref = f32[8,8,128]{2,1,0:T(8,128)S(1)} all-to-all(f32[8,8,128]{2,1,0:T(8,128)S(1)} %get-tuple-element.22), channel_id=1, replica_groups=mesh['ev'=4,'sx'=4,'sz'=8,'sc'=2] {'sx','sc'}, dimensions={0} | all-to-all | bytes 65536 | tf_op jit(solution)/shard_map/all_to_all | solution.py:402
  57.9 0.7 shard_map.39
  58.6 4.0 %all-to-all-start.2 = ((f32[32,8,128]{2,1,0:T(8,128)}), f32[32,8,128]{2,1,0:T(8,128)S(1)}, u32[]{:S(2)}, u32[]{:S(2)}) async-start(f32[32,8,128]{2,1,0:T(8,128)} %shard_map.39), calls=%async_computation.2 | async-start | bytes 262144 | tf_op jit(solution)/shard_map/all_to_all | solution.py:402
  62.6 0.0 copy-start.1
  62.6 2.6 %collective-permute-start.3 = (f32[10,32,128]{2,1,0:T(8,128)S(1)}, f32[10,32,128]{2,1,0:T(8,128)S(1)}, u32[]{:S(2)}, u32[]{:S(2)}) collective-permute-start(f32[10,32,128]{2,1,0:T(8,128)S(1)} %pad_maximum_fusion), channel_id=1, source_target_pairs={{0,192},{64,0},{128,64},{192,128},{1,193},{65,1},{129,65},{193,129... | collective-permute-start | bytes 491528 | tf_op jit(solution)/shard_map/ppermute | solution.py:413
  65.2 6.5 %all-to-all-done.2.x_ref = f32[32,8,128]{2,1,0:T(8,128)S(1)} async-done(((f32[32,8,128]{2,1,0:T(8,128)}), f32[32,8,128]{2,1,0:T(8,128)S(1)}, u32[]{:S(2)}, u32[]{:S(2)}) %all-to-all-start.2) | async-done | bytes 131104 | tf_op jit(solution)/shard_map/all_to_all | solution.py:402
  71.7 0.6 shard_map.40
  72.3 5.3 %all-to-all-start.3 = ((f32[8,8,128]{2,1,0:T(8,128)}), f32[8,8,128]{2,1,0:T(8,128)S(1)}, u32[]{:S(2)}, u32[]{:S(2)}) async-start(f32[8,8,128]{2,1,0:T(8,128)} %shard_map.40), calls=%async_computation.3 | async-start | bytes 65536 | tf_op jit(solution)/shard_map/all_to_all | solution.py:402
  77.6 4.7 %all-to-all-done.3.g0_ref = f32[8,8,128]{2,1,0:T(8,128)S(1)} async-done(((f32[8,8,128]{2,1,0:T(8,128)}), f32[8,8,128]{2,1,0:T(8,128)S(1)}, u32[]{:S(2)}, u32[]{:S(2)}) %all-to-all-start.3) | async-done | bytes 32800 | tf_op jit(solution)/shard_map/all_to_all | solution.py:402
  82.4 3.1 %shard_map.41 = (f32[8,32,128]{2,1,0:T(8,128)S(1)}, f32[1,32,128]{2,1,0:T(8,128)S(1)}, f32[1,32,128]{2,1,0:T(8,128)S(1)}, f32[8,16,128]{2,1,0:T(8,128)}, f32[8,128]{1,0:T(8,128)S(1)}) custom-call(s32[1]{0:T(128)} %bitcast.place_ref, f32[8,8,128]{2,1,0:T(8,128)S(1)} %all-to-all-done.3.g0_ref, f32[32,4096]{1,0:T(8,128)S(1)} %get-tuple-element.23.kt_ref, ...), custom_call_target="tpu_custom_call" | custom-call | flops 1000000 | bytes 1000000 | tf_op jit(solution)/shard_map/pallas_call | solution.py:420
  85.5 4.0 %all-to-all-start.4 = ((f32[8,16,128]{2,1,0:T(8,128)}), f32[8,16,128]{2,1,0:T(8,128)S(1)}, u32[]{:S(2)}, u32[]{:S(2)}) async-start(f32[8,16,128]{2,1,0:T(8,128)} %get-tuple-element.33), calls=%async_computation.4 | async-start | bytes 131072 | tf_op jit(solution)/shard_map/all_to_all | solution.py:402
  89.5 1.0 collective-permute-start.4
  90.5 0.0 collective-permute-start.5
  90.5 2.4 %collective-permute-done.4.edge_ref = f32[1,32,128]{2,1,0:T(8,128)S(1)} collective-permute-done((f32[1,32,128]{2,1,0:T(8,128)S(1)}, f32[1,32,128]{2,1,0:T(8,128)S(1)}, u32[]{:S(2)}, u32[]{:S(2)}) %collective-permute-start.4) | collective-permute-done | bytes 16416 | tf_op jit(solution)/shard_map/ppermute | solution.py:485
  92.9 1.4 %all-to-all-done.4.part_ref = f32[8,16,128]{2,1,0:T(8,128)S(1)} async-done(((f32[8,16,128]{2,1,0:T(8,128)}), f32[8,16,128]{2,1,0:T(8,128)S(1)}, u32[]{:S(2)}, u32[]{:S(2)}) %all-to-all-start.4) | async-done | bytes 65568 | tf_op jit(solution)/shard_map/all_to_all | solution.py:402
  94.4 0.9 shard_map.42
  95.3 3.9 %all-to-all-start.5 = ((f32[32,1,1152]{2,1,0:T(1,128)}), f32[32,1,1152]{2,1,0:T(1,128)S(1)}, u32[]{:S(2)}, u32[]{:S(2)}) async-start(f32[32,1,1152]{2,1,0:T(1,128)} %bitcast.5), calls=%async_computation.5 | async-start | bytes 294912 | tf_op jit(solution)/shard_map/all_to_all | solution.py:402
  99.1 2.9 %collective-permute-start.6 = (f32[10,32,128]{2,1,0:T(8,128)}, f32[10,32,128]{2,1,0:T(8,128)S(1)}, u32[]{:S(2)}, u32[]{:S(2)}) collective-permute-start(f32[10,32,128]{2,1,0:T(8,128)} %copy-done.1), channel_id=1, source_target_pairs={{0,128},{64,192},{128,0},{192,64},{1,129},{65,193},{129,1},{193,65... | collective-permute-start | bytes 491528 | tf_op jit(solution)/shard_map/ppermute | solution.py:413
  102.1 0.9 collective-permute-start.9
  102.9 1.2 collective-permute-start.8
  104.1 1.0 collective-permute-done.6.d2_ref
  105.1 2.5 %collective-permute-done.9.w3_ref = f32[8,32,128]{2,1,0:T(8,128)S(1)} collective-permute-done((f32[8,32,128]{2,1,0:T(8,128)S(1)}, f32[8,32,128]{2,1,0:T(8,128)S(1)}, u32[]{:S(2)}, u32[]{:S(2)}) %collective-permute-start.9) | collective-permute-done | bytes 131104 | tf_op jit(solution)/shard_map/ppermute | solution.py:413
  107.6 1.5 %collective-permute-done.8.w2_ref = f32[8,32,128]{2,1,0:T(8,128)S(1)} collective-permute-done((f32[8,32,128]{2,1,0:T(8,128)S(1)}, f32[8,32,128]{2,1,0:T(8,128)S(1)}, u32[]{:S(2)}, u32[]{:S(2)}) %collective-permute-start.8) | collective-permute-done | bytes 131104 | tf_op jit(solution)/shard_map/ppermute | solution.py:413
  109.1 1.7 %collective-permute-done.7.w1_ref = f32[8,32,128]{2,1,0:T(8,128)S(1)} collective-permute-done((f32[8,32,128]{2,1,0:T(8,128)S(1)}, f32[8,32,128]{2,1,0:T(8,128)S(1)}, u32[]{:S(2)}, u32[]{:S(2)}) %collective-permute-start.7) | collective-permute-done | bytes 131104 | tf_op jit(solution)/shard_map/ppermute | solution.py:413
  110.7 0.1 shard_map.43
  110.9 11.3 %all_to_all.37 = f32[8,1,128]{2,1,0:T(1,128)S(1)} all-to-all(f32[8,1,128]{2,1,0:T(1,128)S(1)} %bitcast.14), channel_id=1, replica_groups=mesh['ev'=4,'sx'=4,'sz'=8,'sc'=2] {'ev','sc'}, dimensions={0} | all-to-all | bytes 8192 | tf_op jit(solution)/shard_map/all_to_all | solution.py:402
  122.2 1.3 %shard_map.44 = f32[8,128,128]{2,1,0:T(8,128)} custom-call(s32[1]{0:T(128)} %bitcast.place_ref, f32[8,128]{1,0:T(8,128)S(1)} %bitcast.13, f32[8,32,128]{2,1,0:T(8,128)S(1)} %get-tuple-element.26.d_ref.d0_ref, f32[10,32,128]{2,1,0:T(8,128)S(1)} %collective-permute-done.2.before_ref.d1_ref, f32[10,32,128]{2,1,0:T(8,128)S(1)} %collective-permute-done.6.d2_ref, ...), custom_call_target="tpu_custom_call" | custom-call | flops 1000000 | bytes 1000000 | tf_op jit(solution)/shard_map/pallas_call | solution.py:420
  (14 shorter events, 0.0 us)
Async XLA Ops:
  45.5 17.0 %collective-permute-start = (f32[2,32,128]{2,1,0:T(8,128)S(1)}, f32[2,32,128]{2,1,0:T(8,128)S(1)}, u32[]{:S(2)}, u32[]{:S(2)}) collective-permute-start(f32[2,32,128]{2,1,0:T(8,128)S(1)} %get-tuple-element.27), channel_id=1, source_target_pairs={{0,1},{1,2},{2,3},{3,4},{4,5},{5,6},{6,7},{7,8},{8,9},{9,10},{10,1... | collective-permute-start | bytes 98312 | tf_op jit(solution)/shard_map/ppermute | solution.py:410
  46.4 16.2 %collective-permute-start.1 = (f32[2,32,128]{2,1,0:T(8,128)S(1)}, f32[2,32,128]{2,1,0:T(8,128)S(1)}, u32[]{:S(2)}, u32[]{:S(2)}) collective-permute-start(f32[2,32,128]{2,1,0:T(8,128)S(1)} %get-tuple-element.28), channel_id=1, source_target_pairs={{0,63},{1,0},{2,1},{3,2},{4,3},{5,4},{6,5},{7,6},{8,7},{9,8},{10,9... | collective-permute-start | bytes 98312 | tf_op jit(solution)/shard_map/ppermute | solution.py:410
  58.6 35.8 %copy-start = (f32[32]{0:T(128)S(1)}, f32[32]{0:T(128)}, u32[]{:S(2)}) copy-start(f32[32]{0:T(128)} %param.5) | copy-start | bytes 388
  58.6 13.1 %all-to-all-start.2 = ((f32[32,8,128]{2,1,0:T(8,128)}), f32[32,8,128]{2,1,0:T(8,128)S(1)}, u32[]{:S(2)}, u32[]{:S(2)}) async-start(f32[32,8,128]{2,1,0:T(8,128)} %shard_map.39), calls=%async_computation.2 | async-start | bytes 262144 | tf_op jit(solution)/shard_map/all_to_all | solution.py:402
  62.6 19.8 %copy-start.1 = (f32[10,32,128]{2,1,0:T(8,128)}, f32[10,32,128]{2,1,0:T(8,128)S(1)}, u32[]{:S(2)}) copy-start(f32[10,32,128]{2,1,0:T(8,128)S(1)} %pad_maximum_fusion) | copy-start | bytes 491524
  62.6 15.0 %collective-permute-start.3 = (f32[10,32,128]{2,1,0:T(8,128)S(1)}, f32[10,32,128]{2,1,0:T(8,128)S(1)}, u32[]{:S(2)}, u32[]{:S(2)}) collective-permute-start(f32[10,32,128]{2,1,0:T(8,128)S(1)} %pad_maximum_fusion), channel_id=1, source_target_pairs={{0,192},{64,0},{128,64},{192,128},{1,193},{65,1},{129,65},{193,129... | collective-permute-start | bytes 491528 | tf_op jit(solution)/shard_map/ppermute | solution.py:413
  65.2 12.5 %collective-permute-start.2 = (f32[10,32,128]{2,1,0:T(8,128)S(1)}, f32[10,32,128]{2,1,0:T(8,128)S(1)}, u32[]{:S(2)}, u32[]{:S(2)}) collective-permute-start(f32[10,32,128]{2,1,0:T(8,128)S(1)} %pad_maximum_fusion), channel_id=1, source_target_pairs={{0,64},{64,128},{128,192},{192,0},{1,65},{65,129},{129,193},{193,1... | collective-permute-start | bytes 491528 | tf_op jit(solution)/shard_map/ppermute | solution.py:413
  72.3 10.0 %all-to-all-start.3 = ((f32[8,8,128]{2,1,0:T(8,128)}), f32[8,8,128]{2,1,0:T(8,128)S(1)}, u32[]{:S(2)}, u32[]{:S(2)}) async-start(f32[8,8,128]{2,1,0:T(8,128)} %shard_map.40), calls=%async_computation.3 | async-start | bytes 65536 | tf_op jit(solution)/shard_map/all_to_all | solution.py:402
  85.5 8.9 %all-to-all-start.4 = ((f32[8,16,128]{2,1,0:T(8,128)}), f32[8,16,128]{2,1,0:T(8,128)S(1)}, u32[]{:S(2)}, u32[]{:S(2)}) async-start(f32[8,16,128]{2,1,0:T(8,128)} %get-tuple-element.33), calls=%async_computation.4 | async-start | bytes 131072 | tf_op jit(solution)/shard_map/all_to_all | solution.py:402
  89.5 3.5 %collective-permute-start.4 = (f32[1,32,128]{2,1,0:T(8,128)S(1)}, f32[1,32,128]{2,1,0:T(8,128)S(1)}, u32[]{:S(2)}, u32[]{:S(2)}) collective-permute-start(f32[1,32,128]{2,1,0:T(8,128)S(1)} %get-tuple-element.30), channel_id=1, source_target_pairs={{0,63},{1,2},{2,1},{3,4},{4,3},{5,6},{6,5},{7,8},{8,7},{9,10},{10,... | collective-permute-start | bytes 49160 | tf_op jit(solution)/shard_map/ppermute | solution.py:485
  90.5 2.4 %collective-permute-start.5 = (f32[1,32,128]{2,1,0:T(8,128)S(1)}, f32[1,32,128]{2,1,0:T(8,128)S(1)}, u32[]{:S(2)}, u32[]{:S(2)}) collective-permute-start(f32[1,32,128]{2,1,0:T(8,128)S(1)} %get-tuple-element.31), channel_id=1, source_target_pairs={{0,1},{1,0},{2,3},{3,2},{4,5},{5,4},{6,7},{7,6},{8,9},{9,8},{10,11... | collective-permute-start | bytes 49160 | tf_op jit(solution)/shard_map/ppermute | solution.py:486
  95.3 15.5 %all-to-all-start.5 = ((f32[32,1,1152]{2,1,0:T(1,128)}), f32[32,1,1152]{2,1,0:T(1,128)S(1)}, u32[]{:S(2)}, u32[]{:S(2)}) async-start(f32[32,1,1152]{2,1,0:T(1,128)} %bitcast.5), calls=%async_computation.5 | async-start | bytes 294912 | tf_op jit(solution)/shard_map/all_to_all | solution.py:402
  99.1 6.0 %collective-permute-start.6 = (f32[10,32,128]{2,1,0:T(8,128)}, f32[10,32,128]{2,1,0:T(8,128)S(1)}, u32[]{:S(2)}, u32[]{:S(2)}) collective-permute-start(f32[10,32,128]{2,1,0:T(8,128)} %copy-done.1), channel_id=1, source_target_pairs={{0,128},{64,192},{128,0},{192,64},{1,129},{65,193},{129,1},{193,65... | collective-permute-start | bytes 491528 | tf_op jit(solution)/shard_map/ppermute | solution.py:413
  102.1 5.5 %collective-permute-start.9 = (f32[8,32,128]{2,1,0:T(8,128)S(1)}, f32[8,32,128]{2,1,0:T(8,128)S(1)}, u32[]{:S(2)}, u32[]{:S(2)}) collective-permute-start(f32[8,32,128]{2,1,0:T(8,128)S(1)} %get-tuple-element.29.w_ref.w0_ref), channel_id=1, source_target_pairs={{0,192},{64,0},{128,64},{192,128},{1,193},{65,1},{129,65},{193,129... | collective-permute-start | bytes 393224 | tf_op jit(solution)/shard_map/ppermute | solution.py:413
  102.9 6.1 %collective-permute-start.8 = (f32[8,32,128]{2,1,0:T(8,128)S(1)}, f32[8,32,128]{2,1,0:T(8,128)S(1)}, u32[]{:S(2)}, u32[]{:S(2)}) collective-permute-start(f32[8,32,128]{2,1,0:T(8,128)S(1)} %get-tuple-element.29.w_ref.w0_ref), channel_id=1, source_target_pairs={{0,128},{64,192},{128,0},{192,64},{1,129},{65,193},{129,1},{193,65... | collective-permute-start | bytes 393224 | tf_op jit(solution)/shard_map/ppermute | solution.py:413
  104.1 6.6 %collective-permute-start.7 = (f32[8,32,128]{2,1,0:T(8,128)S(1)}, f32[8,32,128]{2,1,0:T(8,128)S(1)}, u32[]{:S(2)}, u32[]{:S(2)}) collective-permute-start(f32[8,32,128]{2,1,0:T(8,128)S(1)} %get-tuple-element.29.w_ref.w0_ref), channel_id=1, source_target_pairs={{0,64},{64,128},{128,192},{192,0},{1,65},{65,129},{129,193},{193,1... | collective-permute-start | bytes 393224 | tf_op jit(solution)/shard_map/ppermute | solution.py:413

commit v3 on v2

--- a/solution.py
+++ b/solution.py
@@ -11,6 +11,7 @@
 F32 = jnp.float32
 BF16 = jnp.bfloat16
 I32 = jnp.int32
+
 
 ALL = ("ev", "sx", "sz", "sc")
 SLAB = ("sx", "sz", "sc")
@@ -232,12 +233,7 @@
     return [laplace(f_ref, i)[8:40] for i in range(2, 10)]
 
 
-def second_kernel(
-    place_ref, g0_ref, kt_ref, j_ref, inf_ref, d_ref, below_ref, above_ref, before_ref, after_ref,
-    w_ref, edge_ref, near_ref, g_ref, scal_ref, l_ref, e_ref, f_ref,
-):
-    ev = lax.shift_right_logical(place_ref[0], 6)
-    core = place_ref[0] & 1
+def apply_kernel(g0_ref, kt_ref, j_ref, inf_ref, t_ref, l_ref):
     rays = jnp.concatenate(
         [jnp.concatenate([g0_ref[2 * a], g0_ref[2 * a + 1]], axis=1) for a in range(4)], axis=0
     )
@@ -248,8 +244,16 @@
         )
         for t in range(16)
     ]
-    flat = scatter_rows(kt_ref, j_ref, inf_ref, l_ref, weights)
-    cube = to_cube(flat)
+    t_ref[...] = scatter_rows(kt_ref, j_ref, inf_ref, l_ref, weights)
+
+
+def second_kernel(
+    place_ref, t_ref, kt_ref, j_ref, inf_ref, d_ref, below_ref, above_ref, before_ref, after_ref,
+    w_ref, both_ref, edge_ref, near_ref, g_ref, scal_ref, e_ref, f_ref,
+):
+    ev = lax.shift_right_logical(place_ref[0], 6)
+    core = place_ref[0] & 1
+    cube = to_cube(t_ref[...])
     square = apply_square(ev, d_ref, below_ref, above_ref, before_ref, after_ref, e_ref, f_ref)
     cube = [cube[i] + (damping * damping) * square[i] for i in range(8)]
     dd = jnp.zeros((32, 128), F32)
@@ -258,6 +262,8 @@
     for i in range(8):
         w_ref[i] = cube[i]
         d = d_ref[i]
+        both_ref[i] = d
+        both_ref[8 + i] = cube[i]
         dd = dd + d * d
         dw = dw + d * cube[i]
         ww = ww + cube[i] * cube[i]
@@ -340,10 +346,7 @@
     out_ref[...] = jnp.broadcast_to(row, (8, 128))
 
 
-def final_kernel(
-    place_ref, scal_ref, d0_ref, d1_ref, d2_ref, d3_ref, w0_ref, w1_ref, w2_ref, w3_ref,
-    out_ref, x_ref,
-):
+def coefficient_kernel(scal_ref, out_ref):
     sums = jnp.sum(scal_ref[...], axis=0, keepdims=True)
     lane = iota((1, 128), 1)
 
@@ -388,12 +391,25 @@
     step = phi2 / rho2
     k1 = step * tau
     k0 = phi1 / rho1 * sigma0 - step * (tau * shift + theta1 / rho1 * sigma0)
+    out_ref[0:1] = jnp.broadcast_to(k0, (1, 128))
+    out_ref[1:2] = jnp.broadcast_to(k1, (1, 128))
+
+
+def final_kernel(
+    place_ref, k_ref, d0_ref, d1_ref, d3_ref, w0_ref, w1_ref, w3_ref, both_ref, out_ref, x_ref
+):
+    k0, k1 = k_ref[0:1], k_ref[1:2]
     ev = lax.shift_right_logical(place_ref[0], 6)
-    pairs = ((d0_ref, w0_ref), (d1_ref, w1_ref), (d2_ref, w2_ref), (d3_ref, w3_ref))
-    for n, (d_ref, w_ref) in enumerate(pairs):
+    for n in range(4):
         owner = (ev - n) & 3
+        rows = pl.ds(pl.multiple_of(32 * owner, 32), 32)
         for i in range(8):
-            x_ref[i, pl.ds(pl.multiple_of(32 * owner, 32), 32), :] = k0 * d_ref[i] + k1 * w_ref[i]
+            if n == 2:
+                d, w = both_ref[i], both_ref[8 + i]
+            else:
+                d_ref, w_ref = {0: (d0_ref, w0_ref), 1: (d1_ref, w1_ref), 3: (d3_ref, w3_ref)}[n]
+                d, w = d_ref[i], w_ref[i]
+            x_ref[i, rows, :] = k0 * d + k1 * w
     for i in range(8):
         out_ref[i] = x_ref[i].T
 
@@ -441,8 +457,12 @@
             pltpu.VMEM((1024, 128), F32),
             pltpu.SemaphoreType.DMA((3,)),
         ],
-        compiler_params=pltpu.CompilerParams(vmem_limit_bytes=63 << 20),
-    )(block_ids, delays.reshape(1, 32), kernels.reshape(1024, 128))
+        compiler_params=pltpu.CompilerParams(vmem_limit_bytes=16 << 20),
+    )(
+        pltpu.with_memory_space_constraint(block_ids, pltpu.MemorySpace.HBM),
+        pltpu.with_memory_space_constraint(delays.reshape(1, 32), pltpu.MemorySpace.HBM),
+        pltpu.with_memory_space_constraint(kernels.reshape(1024, 128), pltpu.MemorySpace.HBM),
+    )
     received = exchange(send.reshape(256, 1, 640), ALL).reshape(1280, 128)
 
     cube = ((8, 32, 128), F32)
@@ -463,7 +483,7 @@
     below = slab_shift(d_high, 1)
     above = slab_shift(d_low, -1)
     wide = jnp.concatenate([d0, above[:1], below[1:]], axis=0)
-    d_1, d_2, d_3 = (ev_shift(wide, n) for n in (1, 2, 3))
+    d_1, d_3 = (ev_shift(wide, n) for n in (1, 3))
 
     rays = exchange(rays, D1)
     (rays,) = run(spread_kernel, (rays,), [((32, 8, 128), F32)])
@@ -471,12 +491,17 @@
     (rays,) = run(spread_kernel, (rays,), [((8, 8, 128), F32)])
     rays = exchange(rays, D1)
 
-    w1, w_edge, w_near, rays1, scal = run_ev(
+    (applied,) = run(
+        apply_kernel,
+        (rays, kt, one_hot, info),
+        [((128, 256), F32)],
+        [pltpu.VMEM((256, 4096), BF16)],
+    )
+    w1, both, w_edge, w_near, rays1, scal = run_ev(
         second_kernel,
-        (rays, kt, one_hot, info, d0, below, above, d_1, d_3),
-        [cube, ((1, 32, 128), F32), ((1, 32, 128), F32), ((8, 16, 128), F32), ((8, 128), F32)],
+        (applied, kt, one_hot, info, d0, below, above, d_1, d_3),
+        [cube, ((16, 32, 128), F32), ((1, 32, 128), F32), ((1, 32, 128), F32), ((8, 16, 128), F32), ((8, 128), F32)],
         [
-            pltpu.VMEM((256, 4096), BF16),
             pltpu.VMEM((12, 48, 128), F32),
             pltpu.VMEM((12, 48, 128), F32),
         ],
@@ -491,14 +516,15 @@
         [((288, 128), F32)],
         [pltpu.VMEM((48, 128), F32)],
     )
-    w_1, w_2, w_3 = (ev_shift(w1, n) for n in (1, 2, 3))
+    w_1, w_3 = (ev_shift(w1, n) for n in (1, 3))
+    both_2 = ev_shift(both, 2)
     packed = exchange(packed.reshape(32, 1, 1152), FAR).reshape(288, 128)
-    packed, d_2, w_1, w_2, w_3 = lax.optimization_barrier((packed, d_2, w_1, w_2, w_3))
     (sums,) = run(ray_norm_kernel, (packed,), [((8, 128), F32)])
     sums = exchange(sums.reshape(8, 1, 128), NEAR).reshape(8, 128)
+    (coefs,) = run(coefficient_kernel, (sums,), [((8, 128), F32)])
     (out,) = run_ev(
         final_kernel,
-        (sums, d0, d_1, d_2, d_3, w1, w_1, w_2, w_3),
+        (coefs, d0, d_1, d_3, w1, w_1, w_3, both_2),
         [((8, 128, 128), F32)],
         [pltpu.VMEM((8, 128, 128), F32)],
     )

time: 124 us -> 121 us (0.976)
  Pallas kernels: 12.6 us -> 10.9 us
  waiting for transfers between devices: 21.7 us -> 20.2 us
    ppermute x6 -> x5, waiting for transfers between devices: 6.6 us -> 0.01 us  [ev_shift(): return lax.ppermute(x, 'ev', ring(4, distance))]
    all_to_all x4, waiting for transfers between devices: 12.7 us -> 17.8 us  [exchange(): return lax.all_to_all(x, axes, split_axis=0, concat_axis=0, tiled=True)]
    pallas_call x3, Pallas kernels: 5.35 us -> 3.57 us  [run_ev(): pl.pallas_call(body, out_shape=outs, in_specs=[ev_spec] + [VM] * len(args...]
    pallas_call x4 -> x6, Pallas kernels: 3.96 us -> 4.89 us  [run(): pl.pallas_call(body, out_shape=outs, in_specs=[VM] * len(args), out_specs...]
    ppermute x6 -> x5, starting transfers between devices: 7.58 us -> 6.78 us  [ev_shift(): return lax.ppermute(x, 'ev', ring(4, distance))]
  transfers between devices with their start and end apart: 14 -> 13, of which waited for: 8 -> 5; matrix products, arithmetic and copies ran while one was open for 0% -> 0% of each run, Pallas kernels for 1% -> 2%
where the time goes in v3:
time: 121 us
  blocking collectives  63 us (52%)
  starting transfers between devices  25.9 us (21%)
  waiting for transfers between devices  20.2 us (17%)
  Pallas kernels  10.9 us (9%)
    all_to_all x3, blocking collectives, exchange(): return lax.all_to_all(x, axes, split_axis=0, concat_axis=0, tiled=True)  63 us
    all_to_all x4, waiting for transfers between devices, exchange(): return lax.all_to_all(x, axes, split_axis=0, concat_axis=0, tiled=True)  17.8 us
    all_to_all x4, starting transfers between devices, exchange(): return lax.all_to_all(x, axes, split_axis=0, concat_axis=0, tiled=True)  17.2 us
    ppermute x5, starting transfers between devices, ev_shift(): return lax.ppermute(x, 'ev', ring(4, distance))  6.78 us
    pallas_call x6, Pallas kernels, run(): pl.pallas_call(body, out_shape=outs, in_specs=[VM] * len(args), out_specs...  4.89 us
    pallas_call x3, Pallas kernels, run_ev(): pl.pallas_call(body, out_shape=outs, in_specs=[ev_spec] + [VM] * len(args...  3.57 us
    ppermute x1, waiting for transfers between devices, body(): w_far = lax.ppermute(w_edge, SLAB, pairs)  2.44 us
  transfers between devices with their start and end apart: 13, of which 5 were waited for; matrix products, arithmetic and copies ran while one was open for 0% of the time, Pallas kernels for 2%

profile of v3, /device:TPU:1, one launch (start us, length us, event | category | flops | bytes accessed | tf_op | source)
XLA Modules:
  0.0 120.8 jit_solution(3923123530104568094)
XLA Ops:
  0.0 2.4 %shard_map.37 = f32[1280,128]{1,0:T(8,128)S(1)} custom-call(s32[32,32]{1,0:T(8,128)} %ids_hbm.1, f32[1,32]{1,0:T(1,128)} %bitcast.16, f32[1024,128]{1,0:T(8,128)} %bitcast.18), custom_call_target="tpu_custom_call" | custom-call | tf_op jit(solution)/shard_map/pallas_call | solution.py:448
  2.4 39.5 %all_to_all.35 = f32[256,1,640]{2,1,0:T(1,128)S(1)} all-to-all(f32[256,1,640]{2,1,0:T(1,128)S(1)} %bitcast.12), channel_id=1, replica_groups=mesh['ev'=4,'sx'=4,'sz'=8,'sc'=2] {'ev','sx','sz','sc'}, dimensions={0} | all-to-all | bytes 1310720 | tf_op jit(solution)/shard_map/all_to_all | solution.py:418
  41.9 2.5 %shard_map.38 = (f32[8,32,128]{2,1,0:T(8,128)S(1)}, f32[2,32,128]{2,1,0:T(8,128)S(1)}, f32[2,32,128]{2,1,0:T(8,128)S(1)}, f32[8,8,128]{2,1,0:T(8,128)S(1)}, f32[...) custom-call(f32[1280,128]{1,0:T(8,128)S(1)} %bitcast.11), custom_call_target="tpu_custom_call" | custom-call | flops 1000000 | bytes 1000000 | tf_op jit(solution)/shard_map/pallas_call | solution.py:37
  44.4 0.9 collective-permute-start
  45.3 0.0 collective-permute-start.1
  45.3 11.5 %all_to_all.36.x_ref = f32[8,8,128]{2,1,0:T(8,128)S(1)} all-to-all(f32[8,8,128]{2,1,0:T(8,128)S(1)} %get-tuple-element.18), channel_id=1, replica_groups=mesh['ev'=4,'sx'=4,'sz'=8,'sc'=2] {'sx','sc'}, dimensions={0} | all-to-all | bytes 65536 | tf_op jit(solution)/shard_map/all_to_all | solution.py:418
  56.8 0.7 shard_map.39
  57.5 3.9 %all-to-all-start.2 = ((f32[32,8,128]{2,1,0:T(8,128)}), f32[32,8,128]{2,1,0:T(8,128)S(1)}, u32[]{:S(2)}, u32[]{:S(2)}) async-start(f32[32,8,128]{2,1,0:T(8,128)} %shard_map.39), calls=%async_computation.2 | async-start | bytes 262144 | tf_op jit(solution)/shard_map/all_to_all | solution.py:418
  61.4 0.0 collective-permute-done.1.above_ref
  61.4 2.6 %collective-permute-start.3 = (f32[10,32,128]{2,1,0:T(8,128)S(1)}, f32[10,32,128]{2,1,0:T(8,128)S(1)}, u32[]{:S(2)}, u32[]{:S(2)}) collective-permute-start(f32[10,32,128]{2,1,0:T(8,128)S(1)} %pad_maximum_fusion), channel_id=1, source_target_pairs={{0,192},{64,0},{128,64},{192,128},{1,193},{65,1},{129,65},{193,129... | collective-permute-start | bytes 491528 | tf_op jit(solution)/shard_map/ppermute | solution.py:429
  64.0 6.5 %all-to-all-done.2.x_ref = f32[32,8,128]{2,1,0:T(8,128)S(1)} async-done(((f32[32,8,128]{2,1,0:T(8,128)}), f32[32,8,128]{2,1,0:T(8,128)S(1)}, u32[]{:S(2)}, u32[]{:S(2)}) %all-to-all-start.2) | async-done | bytes 131104 | tf_op jit(solution)/shard_map/all_to_all | solution.py:418
  70.5 0.6 shard_map.40
  71.2 5.3 %all-to-all-start.3 = ((f32[8,8,128]{2,1,0:T(8,128)}), f32[8,8,128]{2,1,0:T(8,128)S(1)}, u32[]{:S(2)}, u32[]{:S(2)}) async-start(f32[8,8,128]{2,1,0:T(8,128)} %shard_map.40), calls=%async_computation.3 | async-start | bytes 65536 | tf_op jit(solution)/shard_map/all_to_all | solution.py:418
  76.5 4.7 %all-to-all-done.3.g0_ref = f32[8,8,128]{2,1,0:T(8,128)S(1)} async-done(((f32[8,8,128]{2,1,0:T(8,128)}), f32[8,8,128]{2,1,0:T(8,128)S(1)}, u32[]{:S(2)}, u32[]{:S(2)}) %all-to-all-start.3) | async-done | bytes 32800 | tf_op jit(solution)/shard_map/all_to_all | solution.py:418
  81.2 0.7 shard_map.41.t_ref
  82.0 0.0 copy-start
  82.0 1.6 %shard_map.42 = (f32[8,32,128]{2,1,0:T(8,128)S(1)}, f32[16,32,128]{2,1,0:T(8,128)S(1)}, f32[1,32,128]{2,1,0:T(8,128)S(1)}, f32[1,32,128]{2,1,0:T(8,128)S(1)}, f3...) custom-call(s32[1]{0:T(128)} %bitcast.place_ref, f32[128,256]{1,0:T(8,128)S(1)} %shard_map.41.t_ref, ...), custom_call_target="tpu_custom_call" | custom-call | flops 1000000 | bytes 1000000 | tf_op jit(solution)/shard_map/pallas_call | solution.py:436
  83.6 0.7 copy-done.1
  84.3 4.0 %all-to-all-start.4 = ((f32[8,16,128]{2,1,0:T(8,128)}), f32[8,16,128]{2,1,0:T(8,128)S(1)}, u32[]{:S(2)}, u32[]{:S(2)}) async-start(f32[8,16,128]{2,1,0:T(8,128)} %get-tuple-element.29), calls=%async_computation.4 | async-start | bytes 131072 | tf_op jit(solution)/shard_map/all_to_all | solution.py:418
  88.3 1.0 collective-permute-start.4
  89.3 2.4 %collective-permute-done.4.edge_ref = f32[1,32,128]{2,1,0:T(8,128)S(1)} collective-permute-done((f32[1,32,128]{2,1,0:T(8,128)S(1)}, f32[1,32,128]{2,1,0:T(8,128)S(1)}, u32[]{:S(2)}, u32[]{:S(2)}) %collective-permute-start.4) | collective-permute-done | bytes 16416 | tf_op jit(solution)/shard_map/ppermute | solution.py:510
  91.7 1.4 %all-to-all-done.4.part_ref = f32[8,16,128]{2,1,0:T(8,128)S(1)} async-done(((f32[8,16,128]{2,1,0:T(8,128)}), f32[8,16,128]{2,1,0:T(8,128)S(1)}, u32[]{:S(2)}, u32[]{:S(2)}) %all-to-all-start.4) | async-done | bytes 65568 | tf_op jit(solution)/shard_map/all_to_all | solution.py:418
  93.1 0.9 shard_map.43
  94.0 4.0 %all-to-all-start.5 = ((f32[32,1,1152]{2,1,0:T(1,128)}), f32[32,1,1152]{2,1,0:T(1,128)S(1)}, u32[]{:S(2)}, u32[]{:S(2)}) async-start(f32[32,1,1152]{2,1,0:T(1,128)} %bitcast.5), calls=%async_computation.5 | async-start | bytes 294912 | tf_op jit(solution)/shard_map/all_to_all | solution.py:418
  98.1 2.7 %collective-permute-start.8 = (f32[16,32,128]{2,1,0:T(8,128)}, f32[16,32,128]{2,1,0:T(8,128)S(1)}, u32[]{:S(2)}, u32[]{:S(2)}) collective-permute-start(f32[16,32,128]{2,1,0:T(8,128)} %copy-done.1), channel_id=1, source_target_pairs={{0,128},{64,192},{128,0},{192,64},{1,129},{65,193},{129,1},{193,65... | collective-permute-start | bytes 786440 | tf_op jit(solution)/shard_map/ppermute | solution.py:429
  100.8 0.9 collective-permute-start.7
  101.7 0.6 collective-permute-start.6
  102.3 5.1 %all-to-all-done.5 = f32[32,1,1152]{2,1,0:T(1,128)S(1)} async-done(((f32[32,1,1152]{2,1,0:T(1,128)}), f32[32,1,1152]{2,1,0:T(1,128)S(1)}, u32[]{:S(2)}, u32[]{:S(2)}) %all-to-all-start.5) | async-done | bytes 147488 | tf_op jit(solution)/shard_map/all_to_all | solution.py:418
  107.4 0.1 shard_map.44
  107.5 12.0 %all_to_all.37 = f32[8,1,128]{2,1,0:T(1,128)S(1)} all-to-all(f32[8,1,128]{2,1,0:T(1,128)S(1)} %bitcast.14), channel_id=1, replica_groups=mesh['ev'=4,'sx'=4,'sz'=8,'sc'=2] {'ev','sc'}, dimensions={0} | all-to-all | bytes 8192 | tf_op jit(solution)/shard_map/all_to_all | solution.py:418
  119.5 0.2 shard_map.45.k_ref
  119.7 1.1 shard_map.46
  (14 shorter events, 0.0 us)
Async XLA Ops:
  44.4 16.9 %collective-permute-start = (f32[2,32,128]{2,1,0:T(8,128)S(1)}, f32[2,32,128]{2,1,0:T(8,128)S(1)}, u32[]{:S(2)}, u32[]{:S(2)}) collective-permute-start(f32[2,32,128]{2,1,0:T(8,128)S(1)} %get-tuple-element.23), channel_id=1, source_target_pairs={{0,1},{1,2},{2,3},{3,4},{4,5},{5,6},{6,7},{7,8},{8,9},{9,10},{10,1... | collective-permute-start | bytes 98312 | tf_op jit(solution)/shard_map/ppermute | solution.py:426
  45.3 16.1 %collective-permute-start.1 = (f32[2,32,128]{2,1,0:T(8,128)S(1)}, f32[2,32,128]{2,1,0:T(8,128)S(1)}, u32[]{:S(2)}, u32[]{:S(2)}) collective-permute-start(f32[2,32,128]{2,1,0:T(8,128)S(1)} %get-tuple-element.24), channel_id=1, source_target_pairs={{0,63},{1,0},{2,1},{3,2},{4,3},{5,4},{6,5},{7,6},{8,7},{9,8},{10,9... | collective-permute-start | bytes 98312 | tf_op jit(solution)/shard_map/ppermute | solution.py:426
  57.5 13.0 %all-to-all-start.2 = ((f32[32,8,128]{2,1,0:T(8,128)}), f32[32,8,128]{2,1,0:T(8,128)S(1)}, u32[]{:S(2)}, u32[]{:S(2)}) async-start(f32[32,8,128]{2,1,0:T(8,128)} %shard_map.39), calls=%async_computation.2 | async-start | bytes 262144 | tf_op jit(solution)/shard_map/all_to_all | solution.py:418
  61.4 20.6 %collective-permute-start.3 = (f32[10,32,128]{2,1,0:T(8,128)S(1)}, f32[10,32,128]{2,1,0:T(8,128)S(1)}, u32[]{:S(2)}, u32[]{:S(2)}) collective-permute-start(f32[10,32,128]{2,1,0:T(8,128)S(1)} %pad_maximum_fusion), channel_id=1, source_target_pairs={{0,192},{64,0},{128,64},{192,128},{1,193},{65,1},{129,65},{193,129... | collective-permute-start | bytes 491528 | tf_op jit(solution)/shard_map/ppermute | solution.py:429
  64.0 18.0 %collective-permute-start.2 = (f32[10,32,128]{2,1,0:T(8,128)S(1)}, f32[10,32,128]{2,1,0:T(8,128)S(1)}, u32[]{:S(2)}, u32[]{:S(2)}) collective-permute-start(f32[10,32,128]{2,1,0:T(8,128)S(1)} %pad_maximum_fusion), channel_id=1, source_target_pairs={{0,64},{64,128},{128,192},{192,0},{1,65},{65,129},{129,193},{193,1... | collective-permute-start | bytes 491528 | tf_op jit(solution)/shard_map/ppermute | solution.py:429
  71.2 10.0 %all-to-all-start.3 = ((f32[8,8,128]{2,1,0:T(8,128)}), f32[8,8,128]{2,1,0:T(8,128)S(1)}, u32[]{:S(2)}, u32[]{:S(2)}) async-start(f32[8,8,128]{2,1,0:T(8,128)} %shard_map.40), calls=%async_computation.3 | async-start | bytes 65536 | tf_op jit(solution)/shard_map/all_to_all | solution.py:418
  82.0 11.2 %copy-start = (f32[32]{0:T(128)S(1)}, f32[32]{0:T(128)}, u32[]{:S(2)}) copy-start(f32[32]{0:T(128)} %param.5) | copy-start | bytes 388
  83.6 0.7 copy-start.1
  84.3 8.9 %all-to-all-start.4 = ((f32[8,16,128]{2,1,0:T(8,128)}), f32[8,16,128]{2,1,0:T(8,128)S(1)}, u32[]{:S(2)}, u32[]{:S(2)}) async-start(f32[8,16,128]{2,1,0:T(8,128)} %get-tuple-element.29), calls=%async_computation.4 | async-start | bytes 131072 | tf_op jit(solution)/shard_map/all_to_all | solution.py:418
  88.3 3.5 %collective-permute-start.4 = (f32[1,32,128]{2,1,0:T(8,128)S(1)}, f32[1,32,128]{2,1,0:T(8,128)S(1)}, u32[]{:S(2)}, u32[]{:S(2)}) collective-permute-start(f32[1,32,128]{2,1,0:T(8,128)S(1)} %get-tuple-element.26), channel_id=1, source_target_pairs={{0,63},{1,2},{2,1},{3,4},{4,3},{5,6},{6,5},{7,8},{8,7},{9,10},{10,... | collective-permute-start | bytes 49160 | tf_op jit(solution)/shard_map/ppermute | solution.py:510
  89.3 2.4 %collective-permute-start.5 = (f32[1,32,128]{2,1,0:T(8,128)S(1)}, f32[1,32,128]{2,1,0:T(8,128)S(1)}, u32[]{:S(2)}, u32[]{:S(2)}) collective-permute-start(f32[1,32,128]{2,1,0:T(8,128)S(1)} %get-tuple-element.27), channel_id=1, source_target_pairs={{0,1},{1,0},{2,3},{3,2},{4,5},{5,4},{6,7},{7,6},{8,9},{9,8},{10,11... | collective-permute-start | bytes 49160 | tf_op jit(solution)/shard_map/ppermute | solution.py:511
  94.0 13.3 %all-to-all-start.5 = ((f32[32,1,1152]{2,1,0:T(1,128)}), f32[32,1,1152]{2,1,0:T(1,128)S(1)}, u32[]{:S(2)}, u32[]{:S(2)}) async-start(f32[32,1,1152]{2,1,0:T(1,128)} %bitcast.5), calls=%async_computation.5 | async-start | bytes 294912 | tf_op jit(solution)/shard_map/all_to_all | solution.py:418
  98.1 21.6 %collective-permute-start.8 = (f32[16,32,128]{2,1,0:T(8,128)}, f32[16,32,128]{2,1,0:T(8,128)S(1)}, u32[]{:S(2)}, u32[]{:S(2)}) collective-permute-start(f32[16,32,128]{2,1,0:T(8,128)} %copy-done.1), channel_id=1, source_target_pairs={{0,128},{64,192},{128,0},{192,64},{1,129},{65,193},{129,1},{193,65... | collective-permute-start | bytes 786440 | tf_op jit(solution)/shard_map/ppermute | solution.py:429
  100.8 18.9 %collective-permute-start.7 = (f32[8,32,128]{2,1,0:T(8,128)S(1)}, f32[8,32,128]{2,1,0:T(8,128)S(1)}, u32[]{:S(2)}, u32[]{:S(2)}) collective-permute-start(f32[8,32,128]{2,1,0:T(8,128)S(1)} %get-tuple-element.25.w_ref.w0_ref), channel_id=1, source_target_pairs={{0,192},{64,0},{128,64},{192,128},{1,193},{65,1},{129,65},{193,129... | collective-permute-start | bytes 393224 | tf_op jit(solution)/shard_map/ppermute | solution.py:429
  101.7 18.0 %collective-permute-start.6 = (f32[8,32,128]{2,1,0:T(8,128)S(1)}, f32[8,32,128]{2,1,0:T(8,128)S(1)}, u32[]{:S(2)}, u32[]{:S(2)}) collective-permute-start(f32[8,32,128]{2,1,0:T(8,128)S(1)} %get-tuple-element.25.w_ref.w0_ref), channel_id=1, source_target_pairs={{0,64},{64,128},{128,192},{192,0},{1,65},{65,129},{129,193},{193,1... | collective-permute-start | bytes 393224 | tf_op jit(solution)/shard_map/ppermute | solution.py:429

commit v4 on v3

--- a/solution.py
+++ b/solution.py
@@ -171,7 +171,7 @@
             g_ref[2 * a + h, 0:8] = total[8 * a : 8 * a + 8, 128 * h : 128 * h + 128]
 
 
-def first_kernel(r_ref, d_ref, low_ref, high_ref, g_ref, kt_ref, j_ref, inf_ref, l_ref):
+def first_kernel(place_ref, r_ref, d_ref, far_ref, near_ref, g_ref, kt_ref, j_ref, inf_ref, l_ref):
     inf_ref[...] = r_ref[pl.ds(4, 256, stride=5), :].T[:64]
     for r in range(4):
         block = r_ref[pl.ds(r, 256, stride=5), :].T
@@ -188,9 +188,10 @@
     cube = to_cube(flat)
     for i in range(8):
         d_ref[i] = cube[i]
+    even = (place_ref[0] & 1) == 0
     for i in range(2):
-        low_ref[i] = cube[i]
-        high_ref[i] = cube[6 + i]
+        far_ref[i] = jnp.where(even, cube[i], cube[6 + i])
+        near_ref[i] = jnp.where(even, cube[6 + i], cube[i])
     gather_rays(flat, kt_ref, j_ref, inf_ref, g_ref)
 
 
@@ -202,24 +203,25 @@
     return up + down
 
 
-def apply_square(ev, d_ref, low_ref, high_ref, before_ref, after_ref, e_ref, f_ref):
+def apply_square(ev, core, d_ref, far_ref, near_ref, before_ref, after_ref, e_ref, f_ref):
     has_low = jnp.where(ev > 0, 1.0, 0.0)
     has_high = jnp.where(ev < 3, 1.0, 0.0)
     for i in range(12):
         if i < 2:
-            own = low_ref[i]
+            own = jnp.where(core == 0, far_ref[i], near_ref[i])
         elif i < 10:
             own = d_ref[i - 2]
         else:
-            own = high_ref[i - 10]
+            own = jnp.where(core == 0, near_ref[i - 10], far_ref[i - 10])
         e_ref[i, 8:40] = own
-    for i in range(1, 11):
-        index = 9 if i == 1 else i - 2
-        e_ref[i, 0:8] = before_ref[index, 24:32] * has_low
-        e_ref[i, 40:48] = after_ref[index, 0:8] * has_high
-    for i in (0, 11):
+    for i in range(12):
         e_ref[i, 0:8] = jnp.zeros((8, 128), F32)
         e_ref[i, 40:48] = jnp.zeros((8, 128), F32)
+    for i in range(1, 11):
+        n = 9 if i == 1 else i - 2
+        for c in range(2):
+            e_ref[i, 6 + c : 7 + c] = before_ref[c, n : n + 1] * has_low
+            e_ref[i, 40 + c : 41 + c] = after_ref[c, n : n + 1] * has_high
     radial = iota((48, 128), 0)
     inside = jnp.where(radial < 8, has_low, jnp.where(radial >= 40, has_high, 1.0))
 
@@ -231,6 +233,20 @@
     for i in range(1, 11):
         f_ref[i] = laplace(e_ref, i) * inside
     return [laplace(f_ref, i)[8:40] for i in range(2, 10)]
+
+
+def strip_kernel(place_ref, d_ref, far_ref, near_ref, low_ref, high_ref):
+    even = (place_ref[0] & 1) == 0
+    above = jnp.where(even, near_ref[0], far_ref[0])
+    below = jnp.where(even, far_ref[1], near_ref[1])
+    for c in range(2):
+        for n in range(16):
+            if n < 8:
+                source = d_ref[n]
+            else:
+                source = above if n == 8 else below
+            low_ref[c, n : n + 1] = source[c : c + 1]
+            high_ref[c, n : n + 1] = source[30 + c : 31 + c]
 
 
 def apply_kernel(g0_ref, kt_ref, j_ref, inf_ref, t_ref, l_ref):
@@ -248,13 +264,13 @@
 
 
 def second_kernel(
-    place_ref, t_ref, kt_ref, j_ref, inf_ref, d_ref, below_ref, above_ref, before_ref, after_ref,
+    place_ref, t_ref, kt_ref, j_ref, inf_ref, d_ref, far_ref, near_in_ref, before_ref, after_ref,
     w_ref, both_ref, edge_ref, near_ref, g_ref, scal_ref, e_ref, f_ref,
 ):
     ev = lax.shift_right_logical(place_ref[0], 6)
     core = place_ref[0] & 1
     cube = to_cube(t_ref[...])
-    square = apply_square(ev, d_ref, below_ref, above_ref, before_ref, after_ref, e_ref, f_ref)
+    square = apply_square(ev, core, d_ref, far_ref, near_in_ref, before_ref, after_ref, e_ref, f_ref)
     cube = [cube[i] + (damping * damping) * square[i] for i in range(8)]
     dd = jnp.zeros((32, 128), F32)
     dw = jnp.zeros((32, 128), F32)
@@ -396,20 +412,17 @@
 
 
 def final_kernel(
-    place_ref, k_ref, d0_ref, d1_ref, d3_ref, w0_ref, w1_ref, w3_ref, both_ref, out_ref, x_ref
+    place_ref, k_ref, d_ref, w_ref, both1_ref, both2_ref, both3_ref, out_ref, x_ref
 ):
     k0, k1 = k_ref[0:1], k_ref[1:2]
     ev = lax.shift_right_logical(place_ref[0], 6)
-    for n in range(4):
-        owner = (ev - n) & 3
-        rows = pl.ds(pl.multiple_of(32 * owner, 32), 32)
+    rows = pl.ds(pl.multiple_of(32 * ev, 32), 32)
+    for i in range(8):
+        x_ref[i, rows, :] = k0 * d_ref[i] + k1 * w_ref[i]
+    for n, both_ref in ((1, both1_ref), (2, both2_ref), (3, both3_ref)):
+        rows = pl.ds(pl.multiple_of(32 * ((ev - n) & 3), 32), 32)
         for i in range(8):
-            if n == 2:
-                d, w = both_ref[i], both_ref[8 + i]
-            else:
-                d_ref, w_ref = {0: (d0_ref, w0_ref), 1: (d1_ref, w1_ref), 3: (d3_ref, w3_ref)}[n]
-                d, w = d_ref[i], w_ref[i]
-            x_ref[i, rows, :] = k0 * d + k1 * w
+            x_ref[i, rows, :] = k0 * both_ref[i] + k1 * both_ref[8 + i]
     for i in range(8):
         out_ref[i] = x_ref[i].T
 
@@ -421,9 +434,6 @@
 def body(kernels, block_ids, delays):
     def ring(count, distance):
         return [(i, (i + distance) % count) for i in range(count)]
-
-    def slab_shift(x, distance):
-        return lax.ppermute(x, SLAB, ring(64, distance))
 
     def ev_shift(x, distance):
         return lax.ppermute(x, "ev", ring(4, distance))
@@ -466,7 +476,7 @@
     received = exchange(send.reshape(256, 1, 640), ALL).reshape(1280, 128)
 
     cube = ((8, 32, 128), F32)
-    d0, d_low, d_high, rays, kt, one_hot, info = run(
+    d0, d_far, d_near, rays, kt, one_hot, info = run_ev(
         first_kernel,
         (received,),
         [
@@ -480,15 +490,17 @@
         ],
         [pltpu.VMEM((256, 4096), BF16)],
     )
-    below = slab_shift(d_high, 1)
-    above = slab_shift(d_low, -1)
-    wide = jnp.concatenate([d0, above[:1], below[1:]], axis=0)
-    d_1, d_3 = (ev_shift(wide, n) for n in (1, 3))
-
+    far_pairs = [(i, (i + 1) % 64 if i % 2 else (i - 1) % 64) for i in range(64)]
+    near_pairs = [(0, 1), (1, 0)]
+    d_far = lax.ppermute(d_far, SLAB, far_pairs)
+    d_near = lax.ppermute(d_near, "sc", near_pairs)
     rays = exchange(rays, D1)
     (rays,) = run(spread_kernel, (rays,), [((32, 8, 128), F32)])
     rays = exchange(rays, D2)
     (rays,) = run(spread_kernel, (rays,), [((8, 8, 128), F32)])
+    low, high = run_ev(strip_kernel, (d0, d_far, d_near), [((2, 16, 128), F32)] * 2)
+    before = ev_shift(high, 1)
+    after = ev_shift(low, -1)
     rays = exchange(rays, D1)
 
     (applied,) = run(
@@ -499,16 +511,15 @@
     )
     w1, both, w_edge, w_near, rays1, scal = run_ev(
         second_kernel,
-        (applied, kt, one_hot, info, d0, below, above, d_1, d_3),
+        (applied, kt, one_hot, info, d0, d_far, d_near, before, after),
         [cube, ((16, 32, 128), F32), ((1, 32, 128), F32), ((1, 32, 128), F32), ((8, 16, 128), F32), ((8, 128), F32)],
         [
             pltpu.VMEM((12, 48, 128), F32),
             pltpu.VMEM((12, 48, 128), F32),
         ],
     )
-    pairs = [(i, (i + 1) % 64 if i % 2 else (i - 1) % 64) for i in range(64)]
-    w_far = lax.ppermute(w_edge, SLAB, pairs)
-    w_near = lax.ppermute(w_near, "sc", [(0, 1), (1, 0)])
+    w_far = lax.ppermute(w_edge, SLAB, far_pairs)
+    w_near = lax.ppermute(w_near, "sc", near_pairs)
     rays1 = exchange(rays1, NEAR)
     (packed,) = run_ev(
         norms_kernel,
@@ -516,15 +527,14 @@
         [((288, 128), F32)],
         [pltpu.VMEM((48, 128), F32)],
     )
-    w_1, w_3 = (ev_shift(w1, n) for n in (1, 3))
-    both_2 = ev_shift(both, 2)
+    both_1, both_2, both_3 = (ev_shift(both, n) for n in (1, 2, 3))
     packed = exchange(packed.reshape(32, 1, 1152), FAR).reshape(288, 128)
     (sums,) = run(ray_norm_kernel, (packed,), [((8, 128), F32)])
     sums = exchange(sums.reshape(8, 1, 128), NEAR).reshape(8, 128)
     (coefs,) = run(coefficient_kernel, (sums,), [((8, 128), F32)])
     (out,) = run_ev(
         final_kernel,
-        (coefs, d0, d_1, d_3, w1, w_1, w_3, both_2),
+        (coefs, d0, w1, both_1, both_2, both_3),
         [((8, 128, 128), F32)],
         [pltpu.VMEM((8, 128, 128), F32)],
     )

time: 121 us -> 118 us (0.975)
  blocking collectives: 63 us -> 18.5 us
  starting transfers between devices: 25.9 us -> 48 us
  waiting for transfers between devices: 20.2 us -> 39.2 us
    all_to_all x3 -> x2, blocking collectives: 63 us -> 18.5 us  [exchange(): return lax.all_to_all(x, axes, split_axis=0, concat_axis=0, tiled=True)]
    all_to_all x4 -> x5, waiting for transfers between devices: 17.8 us -> 38.3 us  [exchange(): return lax.all_to_all(x, axes, split_axis=0, concat_axis=0, tiled=True)]
    all_to_all x4 -> x5, starting transfers between devices: 17.2 us -> 35.2 us  [exchange(): return lax.all_to_all(x, axes, split_axis=0, concat_axis=0, tiled=True)]
    ppermute x4, starting transfers between devices: 1.88 us -> 6.25 us  [the longest x1 2.5 us: body(): w_near = lax.ppermute(w_near, 'sc', near_pairs)]
    pallas_call x3 -> x5, Pallas kernels: 3.57 us -> 6.17 us  [run_ev(): pl.pallas_call(body, out_shape=outs, in_specs=[ev_spec] + [VM] * len(args...]
    pallas_call x6 -> x5, Pallas kernels: 4.89 us -> 2.36 us  [run(): pl.pallas_call(body, out_shape=outs, in_specs=[VM] * len(args), out_specs...]
    ppermute x4, waiting for transfers between devices: 2.44 us -> 0.84 us  [the longest x1 0.66 us: body(): w_far = lax.ppermute(w_edge, SLAB, far_pairs)]
  transfers between devices with their start and end apart: 13 -> 14, of which waited for: 5 -> 7; matrix products, arithmetic and copies ran while one was open for 0% -> 0% of each run, Pallas kernels for 2% -> 1%
where the time goes in v4:
time: 118 us
  starting transfers between devices  48 us (41%)
  waiting for transfers between devices  39.2 us (33%)
  blocking collectives  18.5 us (16%)
  Pallas kernels  11.8 us (10%)
    all_to_all x5, waiting for transfers between devices, exchange(): return lax.all_to_all(x, axes, split_axis=0, concat_axis=0, tiled=True)  38.3 us
    all_to_all x5, starting transfers between devices, exchange(): return lax.all_to_all(x, axes, split_axis=0, concat_axis=0, tiled=True)  35.2 us
    all_to_all x2, blocking collectives, exchange(): return lax.all_to_all(x, axes, split_axis=0, concat_axis=0, tiled=True)  18.5 us
    ppermute x5, starting transfers between devices, ev_shift(): return lax.ppermute(x, 'ev', ring(4, distance))  6.55 us
    pallas_call x5, Pallas kernels, run_ev(): pl.pallas_call(body, out_shape=outs, in_specs=[ev_spec] + [VM] * len(args...  6.17 us
    pallas_call x1, Pallas kernels, body(): pl.pallas_call(prep_kernel, out_shape=jax.ShapeDtypeStruct((1280, 128), F...  3.27 us
    ppermute x1, starting transfers between devices, body(): w_near = lax.ppermute(w_near, 'sc', near_pairs)  2.5 us
  transfers between devices with their start and end apart: 14, of which 7 were waited for; matrix products, arithmetic and copies ran while one was open for 0% of the time, Pallas kernels for 1%

profile of v4, /device:TPU:1, one launch (start us, length us, event | category | flops | bytes accessed | tf_op | source)
XLA Modules:
  0.0 117.6 jit_solution(508909806862918560)
XLA Ops:
  0.0 3.3 %shard_map.37 = f32[1280,128]{1,0:T(8,128)} custom-call(s32[32,32]{1,0:T(8,128)} %ids_hbm.1, f32[1,32]{1,0:T(1,128)} %bitcast.15, f32[1024,128]{1,0:T(8,128)} %bitcast.17), custom_call_target="tpu_custom_call" | custom-call | tf_op jit(solution)/shard_map/pallas_call | solution.py:458
  3.3 15.7 %all-to-all-start = ((f32[256,1,640]{2,1,0:T(1,128)}), f32[256,1,640]{2,1,0:T(1,128)S(1)}, u32[]{:S(2)}, u32[]{:S(2)}) async-start(f32[256,1,640]{2,1,0:T(1,128)} %bitcast.3), calls=%async_computation | async-start | bytes 1310720 | tf_op jit(solution)/shard_map/all_to_all | solution.py:431
  18.9 24.0 %all-to-all-done = f32[256,1,640]{2,1,0:T(1,128)S(1)} async-done(((f32[256,1,640]{2,1,0:T(1,128)}), f32[256,1,640]{2,1,0:T(1,128)S(1)}, u32[]{:S(2)}, u32[]{:S(2)}) %all-to-all-start) | async-done | bytes 655392 | tf_op jit(solution)/shard_map/all_to_all | solution.py:431
  43.0 2.5 %shard_map.38 = (f32[8,32,128]{2,1,0:T(8,128)S(1)}, f32[2,32,128]{2,1,0:T(8,128)S(1)}, f32[2,32,128]{2,1,0:T(8,128)S(1)}, f32[8,8,128]{2,1,0:T(8,128)S(1)}, f32[...) custom-call(s32[1]{0:T(128)} %bitcast.place_ref, f32[1280,128]{1,0:T(8,128)S(1)} %bitcast.11), custom_call_target="tpu_custom_call" | custom-call | flops 1000000 | bytes 1000000 | tf_op jit(solution)/shard_map/pallas_call | solution.py:446
  45.5 7.3 %all_to_all.35.x_ref = f32[8,8,128]{2,1,0:T(8,128)S(1)} all-to-all(f32[8,8,128]{2,1,0:T(8,128)S(1)} %get-tuple-element.20), channel_id=1, replica_groups=mesh['ev'=4,'sx'=4,'sz'=8,'sc'=2] {'sx','sc'}, dimensions={0} | all-to-all | bytes 65536 | tf_op jit(solution)/shard_map/all_to_all | solution.py:431
  52.8 0.7 shard_map.39
  53.4 3.9 %all-to-all-start.2 = ((f32[32,8,128]{2,1,0:T(8,128)}), f32[32,8,128]{2,1,0:T(8,128)S(1)}, u32[]{:S(2)}, u32[]{:S(2)}) async-start(f32[32,8,128]{2,1,0:T(8,128)} %shard_map.39), calls=%async_computation.2 | async-start | bytes 262144 | tf_op jit(solution)/shard_map/all_to_all | solution.py:431
  57.3 2.1 %collective-permute-start = (f32[2,32,128]{2,1,0:T(8,128)S(1)}, f32[2,32,128]{2,1,0:T(8,128)S(1)}, u32[]{:S(2)}, u32[]{:S(2)}) collective-permute-start(f32[2,32,128]{2,1,0:T(8,128)S(1)} %get-tuple-element.25), channel_id=1, source_target_pairs={{0,63},{1,2},{2,1},{3,4},{4,3},{5,6},{6,5},{7,8},{8,7},{9,10},{10,... | collective-permute-start | bytes 98312 | tf_op jit(solution)/shard_map/ppermute | solution.py:495
  59.4 1.3 %collective-permute-start.1 = (f32[2,32,128]{2,1,0:T(8,128)S(1)}, f32[2,32,128]{2,1,0:T(8,128)S(1)}, u32[]{:S(2)}, u32[]{:S(2)}) collective-permute-start(f32[2,32,128]{2,1,0:T(8,128)S(1)} %get-tuple-element.26), channel_id=1, source_target_pairs={{0,1},{1,0},{2,3},{3,2},{4,5},{5,4},{6,7},{7,6},{8,9},{9,8},{10,11... | collective-permute-start | bytes 98312 | tf_op jit(solution)/shard_map/ppermute | solution.py:496
  60.8 5.7 %all-to-all-done.2.x_ref = f32[32,8,128]{2,1,0:T(8,128)S(1)} async-done(((f32[32,8,128]{2,1,0:T(8,128)}), f32[32,8,128]{2,1,0:T(8,128)S(1)}, u32[]{:S(2)}, u32[]{:S(2)}) %all-to-all-start.2) | async-done | bytes 131104 | tf_op jit(solution)/shard_map/all_to_all | solution.py:431
  66.5 0.6 shard_map.40
  67.1 5.8 %all-to-all-start.3 = ((f32[8,8,128]{2,1,0:T(8,128)}), f32[8,8,128]{2,1,0:T(8,128)S(1)}, u32[]{:S(2)}, u32[]{:S(2)}) async-start(f32[8,8,128]{2,1,0:T(8,128)} %shard_map.40), calls=%async_computation.3 | async-start | bytes 65536 | tf_op jit(solution)/shard_map/all_to_all | solution.py:431
  73.0 0.4 collective-permute-start.2
  73.5 2.3 %collective-permute-start.3 = (f32[2,16,128]{2,1,0:T(8,128)S(1)}, f32[2,16,128]{2,1,0:T(8,128)S(1)}, u32[]{:S(2)}, u32[]{:S(2)}) collective-permute-start(f32[2,16,128]{2,1,0:T(8,128)S(1)} %get-tuple-element.28), channel_id=1, source_target_pairs={{0,192},{64,0},{128,64},{192,128},{1,193},{65,1},{129,65},{193,129... | collective-permute-start | bytes 49160 | tf_op jit(solution)/shard_map/ppermute | solution.py:439
  75.8 1.9 %all-to-all-done.3.g0_ref = f32[8,8,128]{2,1,0:T(8,128)S(1)} async-done(((f32[8,8,128]{2,1,0:T(8,128)}), f32[8,8,128]{2,1,0:T(8,128)S(1)}, u32[]{:S(2)}, u32[]{:S(2)}) %all-to-all-start.3) | async-done | bytes 32800 | tf_op jit(solution)/shard_map/all_to_all | solution.py:431
  77.7 0.7 shard_map.41.t_ref
  78.5 1.6 %shard_map.43 = (f32[8,32,128]{2,1,0:T(8,128)S(1)}, f32[16,32,128]{2,1,0:T(8,128)}, f32[1,32,128]{2,1,0:T(8,128)S(1)}, f32[1,32,128]{2,1,0:T(8,128)S(1)}, f32[8,16,128]{2,1,0:T(8,128)}, /*index=5*/f32[8,128]{1,0:T(8,128)S(1)}) custom-call(s32[1]{0:T(128)} %bitcast.place_ref, f32[128,256]{1,0:T(8,128)S(1)} %shard_map.41.t_ref, ...), custom_call_target="tpu_custom_call" | custom-call | flops 1000000 | bytes 1000000 | tf_op jit(solution)/shard_map/pallas_call | solution.py:446
  80.1 4.2 %all-to-all-start.4 = ((f32[8,16,128]{2,1,0:T(8,128)}), f32[8,16,128]{2,1,0:T(8,128)S(1)}, u32[]{:S(2)}, u32[]{:S(2)}) async-start(f32[8,16,128]{2,1,0:T(8,128)} %get-tuple-element.33), calls=%async_computation.4 | async-start | bytes 131072 | tf_op jit(solution)/shard_map/all_to_all | solution.py:431
  84.3 0.3 collective-permute-start.4
  84.6 2.5 %collective-permute-start.5 = (f32[1,32,128]{2,1,0:T(8,128)S(1)}, f32[1,32,128]{2,1,0:T(8,128)S(1)}, u32[]{:S(2)}, u32[]{:S(2)}) collective-permute-start(f32[1,32,128]{2,1,0:T(8,128)S(1)} %get-tuple-element.31), channel_id=1, source_target_pairs={{0,1},{1,0},{2,3},{3,2},{4,5},{5,4},{6,7},{7,6},{8,9},{9,8},{10,11... | collective-permute-start | bytes 49160 | tf_op jit(solution)/shard_map/ppermute | solution.py:522
  87.1 0.7 collective-permute-done.4.edge_ref
  87.7 0.2 collective-permute-done.5.near_ref
  87.9 1.2 %all-to-all-done.4.part_ref = f32[8,16,128]{2,1,0:T(8,128)S(1)} async-done(((f32[8,16,128]{2,1,0:T(8,128)}), f32[8,16,128]{2,1,0:T(8,128)S(1)}, u32[]{:S(2)}, u32[]{:S(2)}) %all-to-all-start.4) | async-done | bytes 65568 | tf_op jit(solution)/shard_map/all_to_all | solution.py:431
  89.1 0.9 shard_map.44
  90.0 5.7 %all-to-all-start.5 = ((f32[32,1,1152]{2,1,0:T(1,128)}), f32[32,1,1152]{2,1,0:T(1,128)S(1)}, u32[]{:S(2)}, u32[]{:S(2)}) async-start(f32[32,1,1152]{2,1,0:T(1,128)} %bitcast.5), calls=%async_computation.5 | async-start | bytes 294912 | tf_op jit(solution)/shard_map/all_to_all | solution.py:431
  95.8 2.6 %collective-permute-start.8 = (f32[16,32,128]{2,1,0:T(8,128)}, f32[16,32,128]{2,1,0:T(8,128)S(1)}, u32[]{:S(2)}, u32[]{:S(2)}) collective-permute-start(f32[16,32,128]{2,1,0:T(8,128)} %get-tuple-element.34), channel_id=1, source_target_pairs={{0,192},{64,0},{128,64},{192,128},{1,193},{65,1},{129,65},{193,129... | collective-permute-start | bytes 786440 | tf_op jit(solution)/shard_map/ppermute | solution.py:439
  98.4 0.6 collective-permute-start.7
  99.0 0.6 collective-permute-start.6
  99.6 5.4 %all-to-all-done.5 = f32[32,1,1152]{2,1,0:T(1,128)S(1)} async-done(((f32[32,1,1152]{2,1,0:T(1,128)}), f32[32,1,1152]{2,1,0:T(1,128)S(1)}, u32[]{:S(2)}, u32[]{:S(2)}) %all-to-all-start.5) | async-done | bytes 147488 | tf_op jit(solution)/shard_map/all_to_all | solution.py:431
  105.1 11.2 %all_to_all.36 = f32[8,1,128]{2,1,0:T(1,128)S(1)} all-to-all(f32[8,1,128]{2,1,0:T(1,128)S(1)} %bitcast.13), channel_id=1, replica_groups=mesh['ev'=4,'sx'=4,'sz'=8,'sc'=2] {'ev','sc'}, dimensions={0} | all-to-all | bytes 8192 | tf_op jit(solution)/shard_map/all_to_all | solution.py:431
  116.3 0.2 shard_map.46.k_ref
  116.5 1.1 shard_map.47
  (11 shorter events, 0.2 us)
Async XLA Ops:
  3.3 39.7 %all-to-all-start = ((f32[256,1,640]{2,1,0:T(1,128)}), f32[256,1,640]{2,1,0:T(1,128)S(1)}, u32[]{:S(2)}, u32[]{:S(2)}) async-start(f32[256,1,640]{2,1,0:T(1,128)} %bitcast.3), calls=%async_computation | async-start | bytes 1310720 | tf_op jit(solution)/shard_map/all_to_all | solution.py:431
  53.4 13.1 %all-to-all-start.2 = ((f32[32,8,128]{2,1,0:T(8,128)}), f32[32,8,128]{2,1,0:T(8,128)S(1)}, u32[]{:S(2)}, u32[]{:S(2)}) async-start(f32[32,8,128]{2,1,0:T(8,128)} %shard_map.39), calls=%async_computation.2 | async-start | bytes 262144 | tf_op jit(solution)/shard_map/all_to_all | solution.py:431
  57.3 15.7 %collective-permute-start = (f32[2,32,128]{2,1,0:T(8,128)S(1)}, f32[2,32,128]{2,1,0:T(8,128)S(1)}, u32[]{:S(2)}, u32[]{:S(2)}) collective-permute-start(f32[2,32,128]{2,1,0:T(8,128)S(1)} %get-tuple-element.25), channel_id=1, source_target_pairs={{0,63},{1,2},{2,1},{3,4},{4,3},{5,6},{6,5},{7,8},{8,7},{9,10},{10,... | collective-permute-start | bytes 98312 | tf_op jit(solution)/shard_map/ppermute | solution.py:495
  59.4 13.6 %collective-permute-start.1 = (f32[2,32,128]{2,1,0:T(8,128)S(1)}, f32[2,32,128]{2,1,0:T(8,128)S(1)}, u32[]{:S(2)}, u32[]{:S(2)}) collective-permute-start(f32[2,32,128]{2,1,0:T(8,128)S(1)} %get-tuple-element.26), channel_id=1, source_target_pairs={{0,1},{1,0},{2,3},{3,2},{4,5},{5,4},{6,7},{7,6},{8,9},{9,8},{10,11... | collective-permute-start | bytes 98312 | tf_op jit(solution)/shard_map/ppermute | solution.py:496
  67.1 10.6 %all-to-all-start.3 = ((f32[8,8,128]{2,1,0:T(8,128)}), f32[8,8,128]{2,1,0:T(8,128)S(1)}, u32[]{:S(2)}, u32[]{:S(2)}) async-start(f32[8,8,128]{2,1,0:T(8,128)} %shard_map.40), calls=%async_computation.3 | async-start | bytes 65536 | tf_op jit(solution)/shard_map/all_to_all | solution.py:431
  73.0 5.5 %collective-permute-start.2 = (f32[2,16,128]{2,1,0:T(8,128)S(1)}, f32[2,16,128]{2,1,0:T(8,128)S(1)}, u32[]{:S(2)}, u32[]{:S(2)}) collective-permute-start(f32[2,16,128]{2,1,0:T(8,128)S(1)} %get-tuple-element.27), channel_id=1, source_target_pairs={{0,64},{64,128},{128,192},{192,0},{1,65},{65,129},{129,193},{193,1... | collective-permute-start | bytes 49160 | tf_op jit(solution)/shard_map/ppermute | solution.py:439
  73.5 5.1 %collective-permute-start.3 = (f32[2,16,128]{2,1,0:T(8,128)S(1)}, f32[2,16,128]{2,1,0:T(8,128)S(1)}, u32[]{:S(2)}, u32[]{:S(2)}) collective-permute-start(f32[2,16,128]{2,1,0:T(8,128)S(1)} %get-tuple-element.28), channel_id=1, source_target_pairs={{0,192},{64,0},{128,64},{192,128},{1,193},{65,1},{129,65},{193,129... | collective-permute-start | bytes 49160 | tf_op jit(solution)/shard_map/ppermute | solution.py:439
  78.5 10.6 %copy-start = (f32[32]{0:T(128)S(1)}, f32[32]{0:T(128)}, u32[]{:S(2)}) copy-start(f32[32]{0:T(128)} %param.5) | copy-start | bytes 388
  80.1 9.0 %all-to-all-start.4 = ((f32[8,16,128]{2,1,0:T(8,128)}), f32[8,16,128]{2,1,0:T(8,128)S(1)}, u32[]{:S(2)}, u32[]{:S(2)}) async-start(f32[8,16,128]{2,1,0:T(8,128)} %get-tuple-element.33), calls=%async_computation.4 | async-start | bytes 131072 | tf_op jit(solution)/shard_map/all_to_all | solution.py:431
  84.3 3.5 %collective-permute-start.4 = (f32[1,32,128]{2,1,0:T(8,128)S(1)}, f32[1,32,128]{2,1,0:T(8,128)S(1)}, u32[]{:S(2)}, u32[]{:S(2)}) collective-permute-start(f32[1,32,128]{2,1,0:T(8,128)S(1)} %get-tuple-element.30), channel_id=1, source_target_pairs={{0,63},{1,2},{2,1},{3,4},{4,3},{5,6},{6,5},{7,8},{8,7},{9,10},{10,... | collective-permute-start | bytes 49160 | tf_op jit(solution)/shard_map/ppermute | solution.py:521
  84.6 3.3 %collective-permute-start.5 = (f32[1,32,128]{2,1,0:T(8,128)S(1)}, f32[1,32,128]{2,1,0:T(8,128)S(1)}, u32[]{:S(2)}, u32[]{:S(2)}) collective-permute-start(f32[1,32,128]{2,1,0:T(8,128)S(1)} %get-tuple-element.31), channel_id=1, source_target_pairs={{0,1},{1,0},{2,3},{3,2},{4,5},{5,4},{6,7},{7,6},{8,9},{9,8},{10,11... | collective-permute-start | bytes 49160 | tf_op jit(solution)/shard_map/ppermute | solution.py:522
  90.0 14.9 %all-to-all-start.5 = ((f32[32,1,1152]{2,1,0:T(1,128)}), f32[32,1,1152]{2,1,0:T(1,128)S(1)}, u32[]{:S(2)}, u32[]{:S(2)}) async-start(f32[32,1,1152]{2,1,0:T(1,128)} %bitcast.5), calls=%async_computation.5 | async-start | bytes 294912 | tf_op jit(solution)/shard_map/all_to_all | solution.py:431
  95.8 20.7 %collective-permute-start.8 = (f32[16,32,128]{2,1,0:T(8,128)}, f32[16,32,128]{2,1,0:T(8,128)S(1)}, u32[]{:S(2)}, u32[]{:S(2)}) collective-permute-start(f32[16,32,128]{2,1,0:T(8,128)} %get-tuple-element.34), channel_id=1, source_target_pairs={{0,192},{64,0},{128,64},{192,128},{1,193},{65,1},{129,65},{193,129... | collective-permute-start | bytes 786440 | tf_op jit(solution)/shard_map/ppermute | solution.py:439
  98.4 18.1 %collective-permute-start.7 = (f32[16,32,128]{2,1,0:T(8,128)}, f32[16,32,128]{2,1,0:T(8,128)S(1)}, u32[]{:S(2)}, u32[]{:S(2)}) collective-permute-start(f32[16,32,128]{2,1,0:T(8,128)} %get-tuple-element.34), channel_id=1, source_target_pairs={{0,128},{64,192},{128,0},{192,64},{1,129},{65,193},{129,1},{193,65... | collective-permute-start | bytes 786440 | tf_op jit(solution)/shard_map/ppermute | solution.py:439
  99.0 17.5 %collective-permute-start.6 = (f32[16,32,128]{2,1,0:T(8,128)}, f32[16,32,128]{2,1,0:T(8,128)S(1)}, u32[]{:S(2)}, u32[]{:S(2)}) collective-permute-start(f32[16,32,128]{2,1,0:T(8,128)} %get-tuple-element.34), channel_id=1, source_target_pairs={{0,64},{64,128},{128,192},{192,0},{1,65},{65,129},{129,193},{193,1... | collective-permute-start | bytes 786440 | tf_op jit(solution)/shard_map/ppermute | solution.py:439
